TPU v7x, 128 devices: a whole 4x4x4 slice. The times are simulated.
128 devices in a mesh: dom: 16 (over y, z), sub: 8 (over x, core).
Axes of the slice: x: 4, y: 4, z: 4, core: 2. Of those that a mesh axis runs over, the one named last changes fastest.
Arguments:
- features: bfloat16 [131072, 256], P(('dom', 'sub')), may hold values from -6 to 6
- cotangent: bfloat16 [131072, 256], P(('dom', 'sub')), may hold values from -6 to 6
- w_self_one: bfloat16 [256, 256], replicated, may hold values from -0.375 to 0.375
- w_nbr_one: bfloat16 [256, 256], replicated, may hold values from -0.375 to 0.375
- bias_one: float32 [256], replicated, may hold values from -4 to 4
- w_self_two: bfloat16 [256, 256], replicated, may hold values from -0.375 to 0.375
- w_nbr_two: bfloat16 [256, 256], replicated, may hold values from -0.375 to 0.375
- in_count: int32 [131072], P(('dom', 'sub')), may hold values from 0 to 7
- send_list: int32 [128, 128, 4], P(('dom', 'sub')), may hold values from 0 to 1023
- src_slot: int32 [128, 2048], P(('dom', 'sub')), may hold values from 0 to 1535
- dst_slot: int32 [128, 2048], P(('dom', 'sub')), may hold values from 0 to 1535
- edge_count: int32 [128], P(('dom', 'sub')), may hold values from 512 to 2048, as said below
Outputs:
- grad_features: bfloat16 [131072, 256], P(('dom', 'sub'))
- grad_weights: float32 [4, 256, 256], replicated
- grad_bias: float32 [256], replicated
Inputs may be any that keep to these rules, and one draw needn't show every extreme that they name: Each device's first edge_count slots are live; one device has all 2048 live in every draw.
All inputs are finite; a program needn't handle non-finite values.
Results may differ from a plain program's by a relative error of at most 0.0056.
Values may be sent and summed in bfloat16 or wider, within the bound.
A program may use at most 64 MiB of HBM per device.

v0:
```python
import math

import jax
import jax.numpy as jnp
from jax import lax
from jax.sharding import PartitionSpec as P


def to_mirrors(master_rows, send_list):
    picked_rows = jnp.take(master_rows, send_list[0], axis=0)
    feature_dim = master_rows.shape[1]
    received = lax.all_to_all(picked_rows, ("dom", "sub"), split_axis=0, concat_axis=0, tiled=True)
    return received.reshape(-1, feature_dim)


def to_masters(mirror_partial, send_list, node_dev):
    feature_dim = mirror_partial.shape[1]
    per_peer = send_list.shape[2]
    sectioned_rows = mirror_partial.reshape(-1, per_peer, feature_dim)
    received = lax.all_to_all(
        sectioned_rows, ("dom", "sub"), split_axis=0, concat_axis=0, tiled=True
    )
    flat_rows = received.reshape(-1, feature_dim)
    owners = send_list[0].reshape(-1)
    placing = (jnp.arange(node_dev, dtype=jnp.int32)[:, None] == owners[None, :]).astype(
        jnp.float32
    )
    return jnp.dot(
        placing, flat_rows, precision=lax.Precision.HIGHEST, preferred_element_type=jnp.float32
    )


def spread(slot_table, from_slot, into_slot, live_count):
    slot_total = slot_table.shape[0]
    edge_slots = from_slot.shape[0]
    feature_dim = slot_table.shape[1]
    block_rows = math.gcd(512, edge_slots)
    slot_ids = jnp.arange(slot_total, dtype=jnp.int32)[None, :]

    def one_block(turn_index, total):
        offset = turn_index * block_rows
        from_part = lax.dynamic_slice_in_dim(from_slot, offset, block_rows)
        into_part = lax.dynamic_slice_in_dim(into_slot, offset, block_rows)
        live_rows = (jnp.arange(block_rows, dtype=jnp.int32) + offset < live_count)[:, None]
        picking = ((from_part[:, None] == slot_ids) & live_rows).astype(slot_table.dtype)
        picked_rows = jnp.dot(picking, slot_table, preferred_element_type=jnp.float32).astype(
            slot_table.dtype
        )
        placing = (into_part[:, None] == slot_ids).astype(slot_table.dtype)
        return total + tdot(placing, picked_rows)

    start_total = jnp.zeros((slot_total, feature_dim), jnp.float32)
    block_count = edge_slots // block_rows
    return lax.fori_loop(0, block_count, one_block, start_total)


def tdot(left, right):
    return lax.dot_general(
        left, right, (((0,), (0,)), ((), ())), preferred_element_type=jnp.float32
    )


def dot_transposed(left, right):
    return lax.dot_general(
        left, right, (((1,), (1,)), ((), ())), preferred_element_type=jnp.float32
    )


def silu_grad(value):
    sigmoid_v = jax.nn.sigmoid(value)
    return sigmoid_v * (1.0 + value * (1.0 - sigmoid_v))


def shards(
    features,
    cotangent,
    w_self_one,
    w_nbr_one,
    bias_one,
    w_self_two,
    w_nbr_two,
    in_count,
    send_list,
    src_slot,
    dst_slot,
    edge_count,
):
    node_dev = features.shape[0]
    sources = src_slot[0]
    targets = dst_slot[0]
    live_count = edge_count[0]
    inverse = (1.0 / jnp.maximum(in_count, 1).astype(jnp.float32))[:, None]

    def gather_sum(master_rows, from_slot, into_slot):
        slot_table = jnp.concatenate([master_rows, to_mirrors(master_rows, send_list)], axis=0)
        partial_value = spread(slot_table, from_slot, into_slot, live_count)
        return partial_value[:node_dev] + to_masters(partial_value[node_dev:], send_list, node_dev)

    mean_one = (gather_sum(features, sources, targets) * inverse).astype(jnp.bfloat16)
    z_one = (
        jnp.dot(features, w_self_one, preferred_element_type=jnp.float32)
        + jnp.dot(mean_one, w_nbr_one, preferred_element_type=jnp.float32)
        + bias_one
    )
    h_one = jax.nn.silu(z_one).astype(jnp.bfloat16)
    message_two = (dot_transposed(cotangent, w_nbr_two) * inverse).astype(jnp.bfloat16)
    forward_sum = gather_sum(h_one, sources, targets)
    backward_sum = gather_sum(message_two, targets, sources)
    mean_two = (forward_sum * inverse).astype(jnp.bfloat16)
    late_self = tdot(h_one, cotangent)
    late_nbr = tdot(mean_two, cotangent)
    grad_h_one = dot_transposed(cotangent, w_self_two) + backward_sum
    grad_z_one = (grad_h_one * silu_grad(z_one)).astype(jnp.bfloat16)
    message_one = (dot_transposed(grad_z_one, w_nbr_one) * inverse).astype(jnp.bfloat16)
    early_self = tdot(features, grad_z_one)
    early_nbr = tdot(mean_one, grad_z_one)
    early_bias = jnp.sum(grad_z_one.astype(jnp.float32), axis=0)
    grad_features = (
        dot_transposed(grad_z_one, w_self_one) + gather_sum(message_one, targets, sources)
    ).astype(jnp.bfloat16)
    self_one, nbr_one, bias_sum, self_two, nbr_two = lax.psum(
        (early_self, early_nbr, early_bias, late_self, late_nbr), ("dom", "sub")
    )
    norm_factor = jnp.float32(node_dev * lax.axis_size("dom") * lax.axis_size("sub")) ** (-0.5)
    grad_weights = jnp.stack([self_one, nbr_one, self_two, nbr_two]) * norm_factor
    grad_bias = bias_sum * norm_factor
    return (grad_features, grad_weights, grad_bias)


def solution(mesh):
    return jax.shard_map(
        shards,
        mesh=mesh,
        in_specs=(
            P(("dom", "sub"), None),
            P(("dom", "sub"), None),
            P(),
            P(),
            P(),
            P(),
            P(),
            P(("dom", "sub")),
            P(("dom", "sub"), None, None),
            P(("dom", "sub"), None),
            P(("dom", "sub"), None),
            P(("dom", "sub")),
        ),
        out_specs=(P(("dom", "sub"), None), P(), P()),
        check_vma=False,
    )
```

profile of v0, /device:TPU:1, one launch (start us, length us, event | category | flops | bytes accessed | tf_op | source)
XLA Modules:
  0.0 453.2 jit_solution(3980596526978102994)
XLA Ops:
  16.2 11.9 %all-to-all-start = ((bf16[128,4,256]{2,1,0:T(4,128)(2,1)}), bf16[128,4,256]{2,1,0:T(4,128)(2,1)}, u32[]{:S(2)}, u32[]{:S(2)}) async-start(bf16[128,4,256]{2,1,0:T(4,128)(2,1)} %get-tuple-element.741), calls=%async_computation | async-start | bytes 524288 | tf_op jit(solution)/shard_map/all_to_all | solution.py:12
  29.0 9.7 %all-to-all-done = bf16[128,4,256]{2,1,0:T(4,128)(2,1)} async-done(((bf16[128,4,256]{2,1,0:T(4,128)(2,1)}), bf16[128,4,256]{2,1,0:T(4,128)(2,1)}, u32[]{:S(2)}, u32[]{:S(2)}) %all-to-all-start) | async-done | bytes 262176 | tf_op jit(solution)/shard_map/all_to_all | solution.py:12
  38.7 4.6 %all-to-all-start.2 = ((bf16[128,4,256]{2,1,0:T(4,128)(2,1)}), bf16[128,4,256]{2,1,0:T(4,128)(2,1)S(1)}, u32[]{:S(2)}, u32[]{:S(2)}) async-start(bf16[128,4,256]{2,1,0:T(4,128)(2,1)} %get-tuple-element.740), calls=%async_computation.2 | async-start | bytes 524288 | tf_op jit(solution)/shard_map/all_to_all | solution.py:12
  46.9 20.3 %while.60 = (s32[]{:T(128)}, f32[1536,256]{1,0:T(8,128)S(1)}, s32[2048]{0:T(1024)S(1)}, s32[2048]{0:T(1024)}, s32[]{:T(128)}, /*index=5*/bf16[1536,256]{1,0:T(8,...) while((s32[]{:T(128)}, f32[1536,256]{1,0:T(8,128)S(1)}, s32[2048]{0:T(1024)S(1)}, ...), condition=%wide.region_1.3_spmd.clone.clone, body=%wide.region_0.0_spmd.clone.clone.sunk | while | flops 808584192 | bytes 3945645 | solution.py:54
  68.7 9.8 %all-to-all-start.1 = ((f32[128,4,256]{2,1,0:T(4,128)}), f32[128,4,256]{2,1,0:T(4,128)S(1)}, u32[]{:S(2)}, u32[]{:S(2)}) async-start(f32[128,4,256]{2,1,0:T(4,128)} %reshape.79), calls=%async_computation.1 | async-start | bytes 1048576 | tf_op jit(solution)/shard_map/all_to_all | solution.py:20
  78.6 22.6 %while.61 = (s32[]{:T(128)}, f32[1536,256]{1,0:T(8,128)}, s32[2048]{0:T(1024)}, s32[2048]{0:T(1024)S(1)}, s32[]{:T(128)}, /*index=5*/bf16[1536,256]{1,0:T(8,128)...) while((s32[]{:T(128)}, f32[1536,256]{1,0:T(8,128)}, s32[2048]{0:T(1024)}, ...), condition=%wide.region_3.5_spmd.clone.clone, body=%wide.region_2.4_spmd.clone.clone.sunk | while | flops 808584192 | bytes 3945645 | solution.py:54
  96.7 4.5 fusion.128
  103.2 9.8 %all-to-all-start.3 = ((f32[128,4,256]{2,1,0:T(4,128)}), f32[128,4,256]{2,1,0:T(4,128)S(1)}, u32[]{:S(2)}, u32[]{:S(2)}) async-start(f32[128,4,256]{2,1,0:T(4,128)} %reshape.82), calls=%async_computation.3 | async-start | bytes 1048576 | tf_op jit(solution)/shard_map/all_to_all | solution.py:20
  117.8 8.8 %all-to-all-done.3 = f32[128,4,256]{2,1,0:T(4,128)S(1)} async-done(((f32[128,4,256]{2,1,0:T(4,128)}), f32[128,4,256]{2,1,0:T(4,128)S(1)}, u32[]{:S(2)}, u32[]{:S(2)}) %all-to-all-start.3) | async-done | bytes 524320 | tf_op jit(solution)/shard_map/all_to_all | solution.py:20
  139.1 4.6 %all-to-all-start.6 = ((bf16[128,4,256]{2,1,0:T(4,128)(2,1)}), bf16[128,4,256]{2,1,0:T(4,128)(2,1)S(1)}, u32[]{:S(2)}, u32[]{:S(2)}) async-start(bf16[128,4,256]{2,1,0:T(4,128)(2,1)} %get-tuple-element.738), calls=%async_computation.6 | async-start | bytes 524288 | tf_op jit(solution)/shard_map/all_to_all | solution.py:12
  144.8 67.1 %psum.39 = f32[256]{0:T(256)S(1)} all-reduce(f32[256]{0:T(256)S(1)} %copy-done.15), channel_id=1, replica_groups=mesh['dom'=16,'sub'=8] {'dom','sub'}, use_global_device_ids=true, to_apply=%region_13.15 | all-reduce | flops 256 | bytes 2048 | tf_op jit(solution)/shard_map/psum | solution.py:121
  212.5 4.7 %all-to-all-start.4 = ((bf16[128,4,256]{2,1,0:T(4,128)(2,1)}), bf16[128,4,256]{2,1,0:T(4,128)(2,1)S(1)}, u32[]{:S(2)}, u32[]{:S(2)}) async-start(bf16[128,4,256]{2,1,0:T(4,128)(2,1)} %get-tuple-element.739), calls=%async_computation.4 | async-start | bytes 524288 | tf_op jit(solution)/shard_map/all_to_all | solution.py:12
  218.2 21.7 %while.63 = (s32[]{:T(128)}, f32[1536,256]{1,0:T(8,128)}, s32[2048]{0:T(1024)S(1)}, s32[2048]{0:T(1024)S(1)}, s32[]{:T(128)}, /*index=5*/bf16[1536,256]{1,0:T(8,...) while((s32[]{:T(128)}, f32[1536,256]{1,0:T(8,128)}, s32[2048]{0:T(1024)S(1)}, ...), condition=%wide.region_10.12_spmd.clone.clone, body=%wide.region_9.11_spmd.clone.clone.sunk | while | flops 808584192 | bytes 3945645 | solution.py:54
  224.0 4.7 %fusion.134 = f32[1536,256]{1,0:T(8,128)} fusion(f32[1536,256]{1,0:T(8,128)} %get-tuple-element.995, s32[512]{0:T(512)S(1)} %dynamic_slice.86, bf16[1536,256]{1,0:T(8,128)(2,1)} %get-tuple-element.1009, s32[512]{0:T(512)S(1)} %dynamic_slice.87, pred[512]{0:T(512)(128)(4,1)S(1)} %add_compare_fusion.11, pred[]{:T(512)S(6)} %compare.15), kind=kOutput, calls=%fused_computation.46.clone.1 | convolution fusion | flops 808583168 | bytes 3936769 | tf_op jit(solution)/shard_map/while/body/eval_jaxpr/dot_general | solution.py:58
  229.6 4.7 %fusion.134 = f32[1536,256]{1,0:T(8,128)} fusion(f32[1536,256]{1,0:T(8,128)} %get-tuple-element.995, s32[512]{0:T(512)S(1)} %dynamic_slice.86, bf16[1536,256]{1,0:T(8,128)(2,1)} %get-tuple-element.1009, s32[512]{0:T(512)S(1)} %dynamic_slice.87, pred[512]{0:T(512)(128)(4,1)S(1)} %add_compare_fusion.11, pred[]{:T(512)S(6)} %compare.15), kind=kOutput, calls=%fused_computation.46.clone.1 | convolution fusion | flops 808583168 | bytes 3936769 | tf_op jit(solution)/shard_map/while/body/eval_jaxpr/dot_general | solution.py:58
  235.1 4.7 %fusion.134 = f32[1536,256]{1,0:T(8,128)} fusion(f32[1536,256]{1,0:T(8,128)} %get-tuple-element.995, s32[512]{0:T(512)S(1)} %dynamic_slice.86, bf16[1536,256]{1,0:T(8,128)(2,1)} %get-tuple-element.1009, s32[512]{0:T(512)S(1)} %dynamic_slice.87, pred[512]{0:T(512)(128)(4,1)S(1)} %add_compare_fusion.11, pred[]{:T(512)S(6)} %compare.15), kind=kOutput, calls=%fused_computation.46.clone.1 | convolution fusion | flops 808583168 | bytes 3936769 | tf_op jit(solution)/shard_map/while/body/eval_jaxpr/dot_general | solution.py:58
  241.9 9.8 %all-to-all-start.7 = ((f32[128,4,256]{2,1,0:T(4,128)}), f32[128,4,256]{2,1,0:T(4,128)S(1)}, u32[]{:S(2)}, u32[]{:S(2)}) async-start(f32[128,4,256]{2,1,0:T(4,128)} %reshape.88), calls=%async_computation.7 | async-start | bytes 1048576 | tf_op jit(solution)/shard_map/all_to_all | solution.py:20
  252.7 21.8 %while.62 = (s32[]{:T(128)}, f32[1536,256]{1,0:T(8,128)}, s32[2048]{0:T(1024)S(1)}, s32[2048]{0:T(1024)S(1)}, s32[]{:T(128)}, /*index=5*/bf16[1536,256]{1,0:T(8,...) while((s32[]{:T(128)}, f32[1536,256]{1,0:T(8,128)}, s32[2048]{0:T(1024)S(1)}, ...), condition=%wide.region_5.7_spmd.clone.clone, body=%wide.region_4.6_spmd.clone.clone.sunk | while | flops 808584192 | bytes 3945645 | solution.py:54
  258.6 4.8 %fusion.131 = f32[1536,256]{1,0:T(8,128)} fusion(f32[1536,256]{1,0:T(8,128)} %get-tuple-element.965, s32[512]{0:T(512)S(1)} %dynamic_slice.84, bf16[1536,256]{1,0:T(8,128)(2,1)} %get-tuple-element.979, s32[512]{0:T(512)S(1)} %dynamic_slice.85, pred[512]{0:T(512)(128)(4,1)S(1)} %add_compare_fusion.10, pred[]{:T(512)S(6)} %compare.14), kind=kOutput, calls=%fused_computation.35.clone.1 | convolution fusion | flops 808583168 | bytes 3936769 | tf_op jit(solution)/shard_map/while/body/eval_jaxpr/dot_general | solution.py:58
  264.1 4.8 %fusion.131 = f32[1536,256]{1,0:T(8,128)} fusion(f32[1536,256]{1,0:T(8,128)} %get-tuple-element.965, s32[512]{0:T(512)S(1)} %dynamic_slice.84, bf16[1536,256]{1,0:T(8,128)(2,1)} %get-tuple-element.979, s32[512]{0:T(512)S(1)} %dynamic_slice.85, pred[512]{0:T(512)(128)(4,1)S(1)} %add_compare_fusion.10, pred[]{:T(512)S(6)} %compare.14), kind=kOutput, calls=%fused_computation.35.clone.1 | convolution fusion | flops 808583168 | bytes 3936769 | tf_op jit(solution)/shard_map/while/body/eval_jaxpr/dot_general | solution.py:58
  269.7 4.8 %fusion.131 = f32[1536,256]{1,0:T(8,128)} fusion(f32[1536,256]{1,0:T(8,128)} %get-tuple-element.965, s32[512]{0:T(512)S(1)} %dynamic_slice.84, bf16[1536,256]{1,0:T(8,128)(2,1)} %get-tuple-element.979, s32[512]{0:T(512)S(1)} %dynamic_slice.85, pred[512]{0:T(512)(128)(4,1)S(1)} %add_compare_fusion.10, pred[]{:T(512)S(6)} %compare.14), kind=kOutput, calls=%fused_computation.35.clone.1 | convolution fusion | flops 808583168 | bytes 3936769 | tf_op jit(solution)/shard_map/while/body/eval_jaxpr/dot_general | solution.py:58
  276.5 9.8 %all-to-all-start.5 = ((f32[128,4,256]{2,1,0:T(4,128)}), f32[128,4,256]{2,1,0:T(4,128)S(1)}, u32[]{:S(2)}, u32[]{:S(2)}) async-start(f32[128,4,256]{2,1,0:T(4,128)} %reshape.85), calls=%async_computation.5 | async-start | bytes 1048576 | tf_op jit(solution)/shard_map/all_to_all | solution.py:20
  291.0 8.9 %all-to-all-done.5 = f32[128,4,256]{2,1,0:T(4,128)S(1)} async-done(((f32[128,4,256]{2,1,0:T(4,128)}), f32[128,4,256]{2,1,0:T(4,128)S(1)}, u32[]{:S(2)}, u32[]{:S(2)}) %all-to-all-start.5) | async-done | bytes 524320 | tf_op jit(solution)/shard_map/all_to_all | solution.py:20
  303.5 140.2 %all-reduce.3.cloned.1.call-done = (f32[1,256,256]{1,2,0:T(8,128)}, f32[1,256,256]{1,2,0:T(8,128)}, f32[1,256,256]{1,2,0:T(8,128)}, f32[1,256,256]{1,2,0:T(8,128)}) async-done(((f32[1,256,256]{1,2,0:T(8,128)}, f32[1,256,256]{1,2,0:T(8,128)}, f32[1,256,256]{1,2,0:T(8,128)}, f32[1,256,256]{1,2,0:T(8,128)}), (f32[1,256,256]{1,2,0:T(8,128)}, f32[1,256,256]{1,2,0:T(8,128)}, f32[1,256,256]{1,2,0:T(8,128)}, ...) | async-done | bytes 1048592 | tf_op jit(solution)/shard_map/psum | solution.py:121
  (158 shorter events, 105.7 us)
Async XLA Ops:
  7.2 2.4 copy-start
  10.8 2.0 copy-start.1
  14.8 13.4 %copy-start.12 = (s32[1,128,4]{1,2,0:T(4,128)S(1)}, s32[1,128,4]{1,2,0:T(4,128)}, u32[]{:S(2)}) copy-start(s32[1,128,4]{1,2,0:T(4,128)} %param.30) | copy-start | bytes 6148
  16.2 30.7 %copy-start.8 = (s32[1,2048]{1,0:T(1,128)S(1)}, s32[1,2048]{1,0:T(1,128)}, u32[]{:S(2)}) copy-start(s32[1,2048]{1,0:T(1,128)} %param.31) | copy-start | bytes 24580
  16.2 22.5 %all-to-all-start = ((bf16[128,4,256]{2,1,0:T(4,128)(2,1)}), bf16[128,4,256]{2,1,0:T(4,128)(2,1)}, u32[]{:S(2)}, u32[]{:S(2)}) async-start(bf16[128,4,256]{2,1,0:T(4,128)(2,1)} %get-tuple-element.741), calls=%async_computation | async-start | bytes 524288 | tf_op jit(solution)/shard_map/all_to_all | solution.py:12
  38.7 29.8 %all-to-all-start.2 = ((bf16[128,4,256]{2,1,0:T(4,128)(2,1)}), bf16[128,4,256]{2,1,0:T(4,128)(2,1)S(1)}, u32[]{:S(2)}, u32[]{:S(2)}) async-start(bf16[128,4,256]{2,1,0:T(4,128)(2,1)} %get-tuple-element.740), calls=%async_computation.2 | async-start | bytes 524288 | tf_op jit(solution)/shard_map/all_to_all | solution.py:12
  67.3 1.4 copy-start.2
  68.7 34.5 %all-to-all-start.1 = ((f32[128,4,256]{2,1,0:T(4,128)}), f32[128,4,256]{2,1,0:T(4,128)S(1)}, u32[]{:S(2)}, u32[]{:S(2)}) async-start(f32[128,4,256]{2,1,0:T(4,128)} %reshape.79), calls=%async_computation.1 | async-start | bytes 1048576 | tf_op jit(solution)/shard_map/all_to_all | solution.py:20
  101.2 11.8 %copy-start.7 = (bf16[256,256]{1,0:T(8,128)(2,1)S(1)}, bf16[256,256]{1,0:T(8,128)(2,1)}, u32[]{:S(2)}) copy-start(bf16[256,256]{1,0:T(8,128)(2,1)} %param.24) | copy-start | bytes 393220
  103.2 23.4 %all-to-all-start.3 = ((f32[128,4,256]{2,1,0:T(4,128)}), f32[128,4,256]{2,1,0:T(4,128)S(1)}, u32[]{:S(2)}, u32[]{:S(2)}) async-start(f32[128,4,256]{2,1,0:T(4,128)} %reshape.82), calls=%async_computation.3 | async-start | bytes 1048576 | tf_op jit(solution)/shard_map/all_to_all | solution.py:20
  113.0 1.5 copy-start.13
  117.8 11.3 %copy-start.4 = (f32[1024,256]{1,0:T(8,128)S(1)}, f32[1024,256]{1,0:T(8,128)}, u32[]{:S(2)}) copy-start(f32[1024,256]{1,0:T(8,128)} %fusion.82) | copy-start | bytes 3145732
  117.8 11.4 %copy-start.11 = (bf16[256,256]{1,0:T(8,128)(2,1)S(1)}, bf16[256,256]{1,0:T(8,128)(2,1)}, u32[]{:S(2)}) copy-start(bf16[256,256]{1,0:T(8,128)(2,1)} %param.25) | copy-start | bytes 393220
  129.2 1.4 copy-start.3
  129.2 1.4 copy-start.16
  137.1 6.6 %copy-start.6 = (bf16[1024,256]{1,0:T(8,128)(2,1)S(1)}, bf16[1024,256]{1,0:T(8,128)(2,1)}, u32[]{:S(2)}) copy-start(bf16[1024,256]{1,0:T(8,128)(2,1)} %copy-done.5) | copy-start | bytes 1572868
  137.2 7.6 %copy-start.15 = (f32[256]{0:T(256)S(1)}, f32[256]{0:T(256)}, u32[]{:S(2)}) copy-start(f32[256]{0:T(256)} %get-tuple-element.744) | copy-start | bytes 3076
  139.1 73.4 %all-to-all-start.6 = ((bf16[128,4,256]{2,1,0:T(4,128)(2,1)}), bf16[128,4,256]{2,1,0:T(4,128)(2,1)S(1)}, u32[]{:S(2)}, u32[]{:S(2)}) async-start(bf16[128,4,256]{2,1,0:T(4,128)(2,1)} %get-tuple-element.738), calls=%async_computation.6 | async-start | bytes 524288 | tf_op jit(solution)/shard_map/all_to_all | solution.py:12
  144.8 73.4 %copy-start.9 = (s32[2048]{0:T(1024)S(1)}, s32[2048]{0:T(1024)}, u32[]{:S(2)}) copy-start(s32[2048]{0:T(1024)} %get-tuple-element.1045) | copy-start | bytes 24580
  212.5 29.4 %all-to-all-start.4 = ((bf16[128,4,256]{2,1,0:T(4,128)(2,1)}), bf16[128,4,256]{2,1,0:T(4,128)(2,1)S(1)}, u32[]{:S(2)}, u32[]{:S(2)}) async-start(bf16[128,4,256]{2,1,0:T(4,128)(2,1)} %get-tuple-element.739), calls=%async_computation.4 | async-start | bytes 524288 | tf_op jit(solution)/shard_map/all_to_all | solution.py:12
  241.9 34.6 %all-to-all-start.7 = ((f32[128,4,256]{2,1,0:T(4,128)}), f32[128,4,256]{2,1,0:T(4,128)S(1)}, u32[]{:S(2)}, u32[]{:S(2)}) async-start(f32[128,4,256]{2,1,0:T(4,128)} %reshape.88), calls=%async_computation.7 | async-start | bytes 1048576 | tf_op jit(solution)/shard_map/all_to_all | solution.py:20
  276.5 11.1 %copy-start.14 = (s32[512]{0:T(512)S(1)}, s32[512]{0:T(512)}, u32[]{:S(2)}) copy-start(s32[512]{0:T(512)} %eq.293) | copy-start | bytes 6148
  276.5 23.4 %all-to-all-start.5 = ((f32[128,4,256]{2,1,0:T(4,128)}), f32[128,4,256]{2,1,0:T(4,128)S(1)}, u32[]{:S(2)}, u32[]{:S(2)}) async-start(f32[128,4,256]{2,1,0:T(4,128)} %reshape.85), calls=%async_computation.5 | async-start | bytes 1048576 | tf_op jit(solution)/shard_map/all_to_all | solution.py:20
  286.3 157.5 %all-reduce.3.cloned.1.call-start = ((), (), s32[]{:S(2)}) async-start(), calls=%async_computation.8 | async-start | bytes 2097152 | tf_op jit(solution)/shard_map/psum | solution.py:121
  (2 other events, 2.5 us)
Sparse Core Ops, SparseCore 0:
  293.1 150.6 all-reduce.2
where the time goes:
time: 455 us; the launch traced here: 453 us
  waiting for transfers between devices  168 us (37%)
  matrix products  88.7 us (19%)
  blocking collectives  67.1 us (15%)
  starting transfers between devices  64.9 us (14%)
  local copies, waits for them, and re-layouts  28.8 us (6%)
  other arithmetic  21.3 us (5%)
  between operations  14.5 us (3%)
    psum x1, waiting for transfers between devices, shards(): lax.psum((early_self, early_nbr, early_bias, late_self, late_nbr), ('dom'...  140 us
    dot_general x20, matrix products, tdot(): lax.dot_general(left, right, (((0,), (0,)), ((), ())), preferred_element_...  72.1 us
    psum x1, blocking collectives, shards(): lax.psum((early_self, early_nbr, early_bias, late_self, late_nbr), ('dom'...  67.1 us
    all_to_all x4, starting transfers between devices, to_masters(): lax.all_to_all(sectioned_rows, ('dom', 'sub'), split_axis=0, concat_axis=...  39.1 us
    all_to_all x4, starting transfers between devices, to_mirrors(): lax.all_to_all(picked_rows, ('dom', 'sub'), split_axis=0, concat_axis=0,...  25.8 us
    all_to_all x4, waiting for transfers between devices, to_masters(): lax.all_to_all(sectioned_rows, ('dom', 'sub'), split_axis=0, concat_axis=...  17.7 us
    lt x16, other arithmetic, one_block(): jnp.arange(block_rows, dtype=jnp.int32) + offset < live_count  10.4 us
    dot_general x4, matrix products, to_masters(): jnp.dot(placing, flat_rows, precision=lax.Precision.HIGHEST, preferred_el...  10.2 us
  transfers between devices with their start and end apart: 9, of which 4 were waited for; matrix products, arithmetic and copies ran while one was open for 25% of the time, Pallas kernels for 0%

commit v1 on v0

v1 whole, which is shorter than its diff:
```python
import functools

import jax
import jax.numpy as jnp
from jax import lax
from jax.experimental import pallas as pl
from jax.experimental.pallas import tpu as pltpu
from jax.sharding import PartitionSpec as P

MESH = pl.DeviceIdType.MESH
F32 = jnp.float32
BF16 = jnp.bfloat16
ONE_HOT = jnp.float8_e4m3fn


def nn(left, right):
    return jnp.dot(left, right, preferred_element_type=F32)


def tn(left, right):
    return lax.dot_general(left, right, (((0,), (0,)), ((), ())), preferred_element_type=F32)


def nt(left, right):
    return lax.dot_general(left, right, (((1,), (1,)), ((), ())), preferred_element_type=F32)


def kernel(
    n_dom,
    n_sub,
    norm_factor,
    count_ref,
    src_ref,
    dst_ref,
    send_ref,
    in_count_ref,
    bias_ref,
    feat_hbm,
    cot_hbm,
    ws1_hbm,
    wn1_hbm,
    ws2_hbm,
    wn2_hbm,
    gfeat_hbm,
    gw_hbm,
    gb_ref,
    feat,
    cot,
    wts,
    src_hot,
    dst_hot,
    adj,
    place,
    inv,
    ybuf,
    zbuf,
    gbuf,
    fown,
    gown,
    hown,
    mbuf,
    hbuf,
    gzbuf,
    send1,
    recv1,
    send2,
    recv2,
    send3,
    recv3,
    send4,
    recv4,
    wpart,
    bpart,
    wpair,
    bpair,
    bsum,
    brecv,
    rs_send,
    rs_recv,
    ag_send,
    ag_all,
    obuf,
    gwbuf,
    in_sem,
    loc_sem,
    ssem,
    rsem,
    out_sem,
):
    nodes, dim = feat.shape
    n_dev = n_dom * n_sub
    n_chip = n_dev // 2
    n_mir = place.shape[1]
    slots = nodes + n_mir
    per_peer = n_mir // n_dev
    half = wpair.shape[0]
    blk = 256
    d = lax.axis_index("dom")
    s = lax.axis_index("sub")
    me = d * n_sub + s
    chip = me // 2
    core = lax.rem(me, 2)
    partner = (d, s + 1 - 2 * core)

    loads = [
        pltpu.make_async_copy(a, b, in_sem.at[i])
        for i, (a, b) in enumerate(
            [
                (feat_hbm, feat),
                (cot_hbm, cot),
                (ws1_hbm, wts.at[0]),
                (wn1_hbm, wts.at[1]),
                (ws2_hbm, wts.at[2]),
                (wn2_hbm, wts.at[3]),
            ]
        )
    ]
    for c in loads:
        c.start()

    def at(p):
        return (p // n_sub, lax.rem(p, n_sub))

    barrier = pltpu.get_barrier_semaphore()

    def greet(i, _):
        pl.semaphore_signal(barrier, 1, device_id=at(lax.rem(me + i, n_dev)), device_id_type=MESH)
        return 0

    lax.fori_loop(1, n_dev, greet, 0)

    def exchange(send, recv, k):
        def one(i, _):
            p = lax.rem(me + i, n_dev)
            pltpu.make_async_remote_copy(
                src_ref=send.at[p],
                dst_ref=recv.at[me],
                send_sem=ssem.at[k],
                recv_sem=rsem.at[k],
                device_id=at(p),
                device_id_type=MESH,
            ).start()
            return 0

        lax.fori_loop(1, n_dev, one, 0)
        pltpu.make_async_copy(send.at[me], recv.at[me], loc_sem.at[k]).start()

    def arrive(send, recv, k):
        pltpu.make_async_copy(send.at[me], recv.at[me], loc_sem.at[k]).wait()
        all_in = recv.at[pl.ds(0, n_dev - 1)]
        pltpu.make_async_copy(all_in, all_in, rsem.at[k]).wait()

    def sent(send, k):
        all_out = send.at[pl.ds(0, n_dev - 1)]
        pltpu.make_async_copy(all_out, all_out, ssem.at[k]).wait()

    def rows(ref, i):
        return ref.at[pl.ds(pl.multiple_of(i * blk, blk), blk), :]

    def mir(ref):
        return ref.reshape(n_mir, dim)

    place[...] = (
        lax.broadcasted_iota(jnp.int32, (nodes, n_mir), 0) == send_ref[...]
    ).astype(BF16)
    inv_row = 1.0 / jnp.maximum(in_count_ref[...], 1).astype(F32)
    inv_col = jnp.broadcast_to(inv_row, (128, nodes)).T
    inv[...] = jnp.concatenate([inv_col] * (dim // 128), axis=1)
    loads[0].wait()
    loads[1].wait()
    ybuf[...] = (cot[...].astype(F32) * inv[...]).astype(BF16)
    send1[:, 0] = tn(place[...], feat[...]).astype(BF16).reshape(n_dev, per_peer, dim)
    send1[:, 1] = tn(place[...], ybuf[...]).astype(BF16).reshape(n_dev, per_peer, dim)

    pl.semaphore_wait(barrier, n_dev - 1)
    exchange(send1, recv1, 0)

    edges = src_ref.shape[1]
    live = lax.broadcasted_iota(jnp.int32, (1, edges), 1) < count_ref[0]
    src_row = jnp.where(live, src_ref[...], -1)
    dst_row = jnp.where(live, dst_ref[...], -1)

    def hot(i, _):
        ids = lax.broadcasted_iota(jnp.int32, (blk, edges), 0) + i * blk
        rows(src_hot, i)[...] = (ids == src_row).astype(ONE_HOT)
        rows(dst_hot, i)[...] = (ids == dst_row).astype(ONE_HOT)
        return 0

    lax.fori_loop(0, slots // blk, hot, 0)

    def build(i, _):
        rows(adj, i)[...] = nt(rows(dst_hot, i)[...], src_hot[...]).astype(BF16)
        return 0

    lax.fori_loop(0, slots // blk, build, 0)

    fown[...] = nn(adj[:, :nodes], feat[...])
    gown[...] = tn(adj[:nodes, :], ybuf[...])
    for c in loads[2:]:
        c.wait()

    arrive(send1, recv1, 0)
    fm = mir(recv1[:, 0])
    gm = mir(recv1[:, 1])
    send2[:, 0] = (
        (fown[nodes:, :] + nn(adj[nodes:, nodes:], fm)).astype(BF16).reshape(n_dev, per_peer, dim)
    )
    send2[:, 1] = (
        (gown[nodes:, :] + tn(adj[nodes:, nodes:], gm)).astype(BF16).reshape(n_dev, per_peer, dim)
    )
    exchange(send2, recv2, 1)
    fown[:nodes, :] += nn(adj[:nodes, nodes:], fm)
    gown[:nodes, :] += tn(adj[nodes:, :nodes], gm)
    zbuf[...] = nn(feat[...], wts[0]) + bias_ref[...]
    gbuf[...] = nt(cot[...], wts[2])

    arrive(send2, recv2, 1)
    fm2 = mir(recv2[:, 0])
    gm2 = mir(recv2[:, 1])

    def dense(i, acc):
        r = pl.multiple_of(i * blk, blk)
        here = pl.ds(r, blk)
        pick = place[here, :]
        scale = inv[here, :]
        mean = ((fown[here, :] + nn(pick, fm2)) * scale).astype(BF16)
        gsum = (gown[here, :] + nn(pick, gm2)).astype(BF16)
        mbuf[here, :] = mean
        gown[here, :] = gsum.astype(F32)
        z = zbuf[here, :] + nn(mean, wts[1])
        gh = gbuf[here, :] + nt(gsum, wts[3])
        sig = 1.0 / (1.0 + jnp.exp(-z))
        hbuf[here, :] = (z * sig).astype(BF16)
        gz = (gh * (sig * (1.0 + z * (1.0 - sig)))).astype(BF16)
        gzbuf[here, :] = gz
        gzf = gz.astype(F32)
        ybuf[here, :] = (gzf * scale).astype(BF16)
        return acc + jnp.sum(gzf, axis=0, keepdims=True)

    bpart[...] = lax.fori_loop(0, nodes // blk, dense, jnp.zeros((1, dim), F32))

    send3[...] = tn(place[...], ybuf[...]).astype(BF16).reshape(n_dev, per_peer, dim)
    exchange(send3, recv3, 2)

    wpart[pl.ds(0, dim), :] = tn(feat[...], gzbuf[...])
    wpart[pl.ds(dim, dim), :] = tn(mbuf[...], gzbuf[...])
    wpart[pl.ds(2 * dim, dim), :] = tn(hbuf[...], cot[...])
    wpart[pl.ds(3 * dim, dim), :] = tn(hbuf[...], gown[:nodes, :].astype(BF16))
    mine = pl.ds(pl.multiple_of(core * half, half), half)
    other = pl.ds(pl.multiple_of((1 - core) * half, half), half)
    pair_w = pltpu.make_async_remote_copy(
        src_ref=wpart.at[other, :],
        dst_ref=wpair,
        send_sem=ssem.at[4],
        recv_sem=rsem.at[4],
        device_id=partner,
        device_id_type=MESH,
    )
    pair_b = pltpu.make_async_remote_copy(
        src_ref=bpart,
        dst_ref=bpair,
        send_sem=ssem.at[5],
        recv_sem=rsem.at[5],
        device_id=partner,
        device_id_type=MESH,
    )
    pair_w.start()
    pair_b.start()

    hown[...] = tn(adj[:nodes, :], ybuf[...])

    pair_w.wait()
    pair_b.wait()
    rs_send[...] = (wpart[mine, :] + wpair[...]).astype(rs_send.dtype).reshape(n_chip, 8, dim)
    bsum[...] = bpart[...] + bpair[...]

    def scatter(i, _):
        q = lax.rem(chip + i, n_chip)
        to = at(q * 2 + core)
        pltpu.make_async_remote_copy(
            src_ref=rs_send.at[q],
            dst_ref=rs_recv.at[chip],
            send_sem=ssem.at[6],
            recv_sem=rsem.at[6],
            device_id=to,
            device_id_type=MESH,
        ).start()
        pltpu.make_async_remote_copy(
            src_ref=bsum,
            dst_ref=brecv.at[chip],
            send_sem=ssem.at[7],
            recv_sem=rsem.at[7],
            device_id=to,
            device_id_type=MESH,
        ).start()
        return 0

    lax.fori_loop(1, n_chip, scatter, 0)
    own_rs = pltpu.make_async_copy(rs_send.at[chip], rs_recv.at[chip], loc_sem.at[4])
    own_rs.start()
    own_b = pltpu.make_async_copy(bsum, brecv.at[chip], loc_sem.at[5])
    own_b.start()

    arrive(send3, recv3, 2)
    hm = mir(recv3[...])
    send4[...] = (
        (hown[nodes:, :] + tn(adj[nodes:, nodes:], hm)).astype(BF16).reshape(n_dev, per_peer, dim)
    )
    exchange(send4, recv4, 3)
    hown[:nodes, :] += tn(adj[nodes:, :nodes], hm)
    zbuf[...] = nt(gzbuf[...], wts[0])

    own_rs.wait()
    own_b.wait()
    others = rs_recv.at[pl.ds(0, n_chip - 1)]
    pltpu.make_async_copy(others, others, rsem.at[6]).wait()
    others = brecv.at[pl.ds(0, n_chip - 1)]
    pltpu.make_async_copy(others, others, rsem.at[7]).wait()
    ag_send[...] = (jnp.sum(rs_recv[...].astype(F32), axis=0) * norm_factor).astype(ag_send.dtype)
    gb_ref[...] = jnp.sum(brecv[...], axis=0) * norm_factor

    def gather(i, _):
        q = lax.rem(chip + i, n_chip)
        pltpu.make_async_remote_copy(
            src_ref=ag_send,
            dst_ref=ag_all.at[core, chip],
            send_sem=ssem.at[8],
            recv_sem=rsem.at[8],
            device_id=at(q * 2 + core),
            device_id_type=MESH,
        ).start()
        return 0

    lax.fori_loop(1, n_chip, gather, 0)
    own_ag = pltpu.make_async_copy(ag_send, ag_all.at[core, chip], loc_sem.at[6])
    own_ag.start()

    arrive(send4, recv4, 3)
    hm2 = mir(recv4[...])

    def last(i, _):
        here = pl.ds(pl.multiple_of(i * blk, blk), blk)
        hsum = (hown[here, :] + nn(place[here, :], hm2)).astype(BF16)
        obuf[here, :] = (zbuf[here, :] + nt(hsum, wts[1])).astype(BF16)
        return 0

    lax.fori_loop(0, nodes // blk, last, 0)
    put = pltpu.make_async_copy(obuf, gfeat_hbm, out_sem.at[0])
    put.start()

    own_ag.wait()
    others = ag_all.at[core, pl.ds(0, n_chip - 1)]
    pltpu.make_async_copy(others, others, rsem.at[8]).wait()
    swap = pltpu.make_async_remote_copy(
        src_ref=ag_all.at[core],
        dst_ref=ag_all.at[core],
        send_sem=ssem.at[9],
        recv_sem=rsem.at[9],
        device_id=partner,
        device_id_type=MESH,
    )
    swap.start()
    swap.wait()
    gwbuf[...] = ag_all[...].astype(F32).reshape(4 * dim, dim)
    put_w = pltpu.make_async_copy(gwbuf, gw_hbm, out_sem.at[1])
    put_w.start()

    sent(send1, 0)
    sent(send2, 1)
    sent(send3, 2)
    sent(send4, 3)
    for ref, k in ((rs_send, 6), (brecv, 7)):
        others = ref.at[pl.ds(0, n_chip - 1)]
        pltpu.make_async_copy(others, others, ssem.at[k]).wait()
    others = ag_all.at[core, pl.ds(0, n_chip - 1)]
    pltpu.make_async_copy(others, others, ssem.at[8]).wait()
    put.wait()
    put_w.wait()


def shards(
    n_dom,
    n_sub,
    features,
    cotangent,
    w_self_one,
    w_nbr_one,
    bias_one,
    w_self_two,
    w_nbr_two,
    in_count,
    send_list,
    src_slot,
    dst_slot,
    edge_count,
):
    nodes, dim = features.shape
    n_dev = n_dom * n_sub
    n_chip = n_dev // 2
    per_peer = send_list.shape[2]
    n_mir = n_dev * per_peer
    slots = nodes + n_mir
    edges = src_slot.shape[1]
    vm = pl.BlockSpec(memory_space=pltpu.VMEM)
    sm = pl.BlockSpec(memory_space=pltpu.SMEM)
    hbm = pl.BlockSpec(memory_space=pl.ANY)
    norm_factor = float(nodes * n_dev) ** -0.5
    msg2 = pltpu.VMEM((n_dev, 2, per_peer, dim), BF16)
    msg1 = pltpu.VMEM((n_dev, per_peer, dim), BF16)
    full = pltpu.VMEM((nodes, dim), F32)
    fullb = pltpu.VMEM((nodes, dim), BF16)
    allf = pltpu.VMEM((slots, dim), F32)
    rs_t = BF16
    ag_t = BF16
    gfeat, gw, gb = pl.pallas_call(
        functools.partial(kernel, n_dom, n_sub, norm_factor),
        out_shape=(
            jax.ShapeDtypeStruct((nodes, dim), BF16),
            jax.ShapeDtypeStruct((4 * dim, dim), F32),
            jax.ShapeDtypeStruct((1, dim), F32),
        ),
        in_specs=[sm, vm, vm, vm, vm, vm, hbm, hbm, hbm, hbm, hbm, hbm],
        out_specs=(hbm, hbm, vm),
        scratch_shapes=[
            fullb,
            fullb,
            pltpu.VMEM((4, dim, dim), BF16),
            pltpu.VMEM((slots, edges), ONE_HOT),
            pltpu.VMEM((slots, edges), ONE_HOT),
            pltpu.VMEM((slots, slots), BF16),
            pltpu.VMEM((nodes, n_mir), BF16),
            full,
            fullb,
            full,
            full,
            allf,
            allf,
            allf,
            fullb,
            fullb,
            fullb,
            msg2,
            msg2,
            msg2,
            msg2,
            msg1,
            msg1,
            msg1,
            msg1,
            pltpu.VMEM((4 * dim, dim), F32),
            pltpu.VMEM((1, dim), F32),
            pltpu.VMEM((2 * dim, dim), F32),
            pltpu.VMEM((1, dim), F32),
            pltpu.VMEM((1, dim), F32),
            pltpu.VMEM((n_chip, 1, dim), F32),
            pltpu.VMEM((n_chip, 2 * dim // n_chip, dim), rs_t),
            pltpu.VMEM((n_chip, 2 * dim // n_chip, dim), rs_t),
            pltpu.VMEM((2 * dim // n_chip, dim), ag_t),
            pltpu.VMEM((2, n_chip, 2 * dim // n_chip, dim), ag_t),
            fullb,
            pltpu.VMEM((4 * dim, dim), F32),
            pltpu.SemaphoreType.DMA((6,)),
            pltpu.SemaphoreType.DMA((7,)),
            pltpu.SemaphoreType.DMA((10,)),
            pltpu.SemaphoreType.DMA((10,)),
            pltpu.SemaphoreType.DMA((2,)),
        ],
        compiler_params=pltpu.CompilerParams(
            collective_id=0, has_side_effects=True, vmem_limit_bytes=60 << 20
        ),
    )(
        edge_count,
        src_slot,
        dst_slot,
        send_list.reshape(1, n_mir),
        in_count.reshape(1, nodes),
        bias_one.reshape(1, dim),
        features,
        cotangent,
        w_self_one,
        w_nbr_one,
        w_self_two,
        w_nbr_two,
    )
    return gfeat, gw.reshape(4, dim, dim), gb.reshape(dim)


def solution(mesh):
    both = ("dom", "sub")
    return jax.shard_map(
        functools.partial(shards, mesh.shape["dom"], mesh.shape["sub"]),
        mesh=mesh,
        in_specs=(
            P(both, None),
            P(both, None),
            P(),
            P(),
            P(),
            P(),
            P(),
            P(both),
            P(both, None, None),
            P(both, None),
            P(both, None),
            P(both),
        ),
        out_specs=(P(both, None), P(), P()),
        check_vma=False,
    )
```

time: 455 us -> 67.2 us (0.15)
  waiting for transfers between devices: 168 us -> 0 us
  matrix products: 88.7 us -> 0 us
  blocking collectives: 67.1 us -> 0 us
  starting transfers between devices: 64.9 us -> 0 us
  Pallas kernels: 0 us -> 60.7 us
  local copies, waits for them, and re-layouts: 28.8 us -> 4.97 us
  other arithmetic: 21.3 us -> 0 us
  between operations: 14.5 us -> 1.31 us
    psum x1 -> x0, waiting for transfers between devices: 140 us -> none  [shards(): lax.psum((early_self, early_nbr, early_bias, late_self, late_nbr), ('dom'...]
    dot_general x30 -> x0, matrix products: 88.7 us -> none  [the longest x20 72.1 us: tdot(): lax.dot_general(left, right, (((0,), (0,)), ((), ())), preferred_element_...]
    psum x1 -> x0, blocking collectives: 67.1 us -> none  [shards(): lax.psum((early_self, early_nbr, early_bias, late_self, late_nbr), ('dom'...]
    all_to_all x8 -> x0, starting transfers between devices: 64.9 us -> none  [the longest x4 39.1 us: to_masters(): lax.all_to_all(sectioned_rows, ('dom', 'sub'), split_axis=0, concat_axis=...]
    pallas_call x0 -> x1, Pallas kernels: none -> 60.7 us  [shards(): pl.pallas_call(functools.partial(kernel, n_dom, n_sub, norm_factor), out_...]
    all_to_all x8 -> x0, waiting for transfers between devices: 27.4 us -> none  [the longest x4 17.7 us: to_masters(): lax.all_to_all(sectioned_rows, ('dom', 'sub'), split_axis=0, concat_axis=...]
    lt x16 -> x0, other arithmetic: 10.4 us -> none  [one_block(): jnp.arange(block_rows, dtype=jnp.int32) + offset < live_count]
    gather x8 -> x0, local copies, waits for them, and re-layouts: 8.08 us -> none  [to_mirrors(): picked_rows = jnp.take(master_rows, send_list[0], axis=0)]
  transfers between devices with their start and end apart: 9 -> 0, of which waited for: 4 -> 0; matrix products, arithmetic and copies ran while one was open for 25% -> 0% of each run, Pallas kernels for 0% -> 0%
where the time goes in v1:
time: 67.2 us; the launch traced here: 67 us
  Pallas kernels  60.7 us (90%)
  local copies, waits for them, and re-layouts  4.97 us (7%)
  between operations  1.31 us (2%)
    pallas_call x1, Pallas kernels, shards(): pl.pallas_call(functools.partial(kernel, n_dom, n_sub, norm_factor), out_...  60.7 us
    unnamed x10, local copies, waits for them, and re-layouts  4.28 us

profile of v1, /device:TPU:1, one launch (start us, length us, event | category | flops | bytes accessed | tf_op | source)
XLA Modules:
  0.0 67.0 jit_solution(6960130825088563763)
XLA Ops:
  1.3 0.0 copy-start.1
  1.3 0.7 %copy-done.1 = s32[1,128,4]{1,2,0:T(4,128)S(1)} copy-done((s32[1,128,4]{1,2,0:T(4,128)S(1)}, s32[1,128,4]{1,2,0:T(4,128)}, u32[]{:S(2)}) %copy-start.1) | copy-done | bytes 2072
  2.0 0.1 copy.16
  2.1 0.7 %reshape.21.send_ref = s32[1,512]{1,0:T(1,128)} reshape(s32[1,128,4]{2,1,0:T(8,128)S(1)} %copy.16) | data formatting | bytes 4096 | tf_op jit(solution)/shard_map/reshape | solution.py:475
  2.8 60.7 %shard_map.139 = (bf16[1024,256]{1,0:T(8,128)(2,1)}, f32[1024,256]{1,0:T(8,128)}, f32[1,256]{1,0:T(1,128)}) custom-call(s32[1]{0:T(128)S(6)} %copy.20.count_ref, s32[1,2048]{1,0:T(1,128)} %src_ref.1, s32[1,2048]{1,0:T(1,128)} %dst_ref.1, s32[1,512]{1,0:T(1,128)} %reshape.21.send_ref, s32[1,1024]{1,0:T(1,128)} %bitcast.5, f32[1,256]{1,0:T(1,128)} %bitcast.6, ...), custom_call_target="tpu_custom_call" | custom-call | tf_op jit(solution)/shard_map/pallas_call | solution.py:415
  63.5 0.0 copy-start
  63.5 2.0 %copy.21 = bf16[1024,256]{1,0:T(8,128)(2,1)} copy(bf16[1024,256]{1,0:T(8,128)(2,1)} %get-tuple-element.12) | data formatting | bytes 1048576
  65.5 0.0 copy-done
  65.5 0.0 copy-start.2
  65.5 1.0 %copy.22 = f32[4,256,256]{2,1,0:T(8,128)} copy(f32[4,256,256]{2,1,0:T(8,128)S(1)} %bitcast.4) | data formatting | bytes 2097152
  66.5 0.0 copy-done.2
  66.5 0.6 copy.23
Async XLA Ops:
  1.3 0.7 %copy-start.1 = (s32[1,128,4]{1,2,0:T(4,128)S(1)}, s32[1,128,4]{1,2,0:T(4,128)}, u32[]{:S(2)}) copy-start(s32[1,128,4]{1,2,0:T(4,128)} %param.20) | copy-start | bytes 6148
  63.5 2.0 %copy-start = (f32[1024,256]{1,0:T(8,128)S(1)}, f32[1024,256]{1,0:T(8,128)}, u32[]{:S(2)}) copy-start(f32[1024,256]{1,0:T(8,128)} %get-tuple-element.7) | copy-start | bytes 3145732
  65.5 1.0 %copy-start.2 = (f32[1,256]{1,0:T(1,128)S(1)}, f32[1,256]{1,0:T(1,128)}, u32[]{:S(2)}) copy-start(f32[1,256]{1,0:T(1,128)} %get-tuple-element.8) | copy-start | bytes 3076

commit v2 on v1

v2 whole, which is shorter than its diff:
```python
import contextlib
import functools

import jax
import jax.numpy as jnp
from jax import lax
from jax.experimental import pallas as pl
from jax.experimental.pallas import tpu as pltpu
from jax.sharding import PartitionSpec as P

MESH = pl.DeviceIdType.MESH
F32 = jnp.float32
BF16 = jnp.bfloat16
ONE_HOT = jnp.float8_e4m3fn
FAR = (10, 9, 11, 6, 14, 8, 2, 5, 7, 13, 15, 4, 12, 1, 3)


def scope(name):
    return contextlib.nullcontext()


def nn(left, right):
    return jnp.dot(left, right, preferred_element_type=F32)


def tn(left, right):
    return lax.dot_general(left, right, (((0,), (0,)), ((), ())), preferred_element_type=F32)


def nt(left, right):
    return lax.dot_general(left, right, (((1,), (1,)), ((), ())), preferred_element_type=F32)


def digits(codes):
    total = 0
    for code in reversed(codes):
        total = total * 16 + code
    return total


def wrap4(v):
    return jnp.where(v >= 4, v - 4, v)


def kernel(
    n_dom,
    n_sub,
    norm_factor,
    count_hbm,
    src_hbm,
    dst_hbm,
    send_hbm,
    in_count_hbm,
    bias_hbm,
    feat_hbm,
    cot_hbm,
    ws1_hbm,
    wn1_hbm,
    ws2_hbm,
    wn2_hbm,
    gfeat_ref,
    gw_ref,
    gb_ref,
    count_ref,
    src_ref,
    dst_ref,
    send_ref,
    in_count_ref,
    bias_ref,
    feat,
    cot,
    wts,
    src_hot,
    dst_hot,
    adj,
    place,
    inv,
    ybuf,
    zbuf,
    gbuf,
    fown,
    gown,
    hown,
    mbuf,
    hbuf,
    gzbuf,
    sends,
    recvs,
    wpart,
    bpart,
    wpair,
    bpair,
    bsum,
    brecv,
    rs_send,
    rs_recv,
    ag_send,
    ag_all,
    in_sem,
    loc_sem,
    ssem,
    rsem,
):
    nodes, dim = feat.shape
    n_dev = n_dom * n_sub
    n_chip = n_dev // 2
    n_mir = place.shape[1]
    slots = nodes + n_mir
    per_peer = n_mir // n_dev
    half = wpair.shape[0]
    blk = 256
    d = lax.axis_index("dom")
    s = lax.axis_index("sub")
    me = d * n_sub + s
    chip = lax.div(me, 2)
    core = lax.rem(me, 2)
    at_y, at_z, at_x = lax.div(d, 4), lax.rem(d, 4), lax.div(s, 2)
    partner = (d, s + 1 - 2 * core)

    small = [
        (send_hbm, send_ref),
        (in_count_hbm, in_count_ref),
        (count_hbm, count_ref),
        (src_hbm, src_ref),
        (dst_hbm, dst_ref),
        (bias_hbm, bias_ref),
    ]
    large = [
        (feat_hbm, feat),
        (cot_hbm, cot),
        (ws1_hbm, wts.at[0]),
        (wn1_hbm, wts.at[1]),
        (ws2_hbm, wts.at[2]),
        (wn2_hbm, wts.at[3]),
    ]
    loads = [
        pltpu.make_async_copy(a, b, in_sem.at[i]) for i, (a, b) in enumerate(small + large)
    ]
    for c in loads:
        c.start()

    xs = [wrap4(at_x + k) * 2 for k in (2, 1, 3, 0)]
    cores = [1 - core, core]

    def each(do, both):
        def line(dom, is_mine):
            for k in range(4):
                for j in range(2):
                    if (both or j == 1) and not (is_mine and k == 3 and j == 1):
                        do(dom, xs[k] + cores[j])

        def dom_of(code):
            return wrap4(at_y + lax.div(code, 4)) * 4 + wrap4(at_z + lax.rem(code, 4))

        def turn(_, left):
            line(dom_of(lax.rem(left, 16)), False)
            return lax.div(left, 16)

        lax.fori_loop(0, 7, turn, jnp.int32(digits(FAR[:7])))
        lax.fori_loop(0, 7, turn, jnp.int32(digits(FAR[7:14])))
        line(dom_of(jnp.int32(FAR[14])), False)
        line(d, True)

    barrier = pltpu.get_barrier_semaphore()
    with scope("greet"):
        each(
            lambda a, b: pl.semaphore_signal(barrier, 1, device_id=(a, b), device_id_type=MESH),
            True,
        )

    def exchange(k):
        def one(a, b):
            pltpu.make_async_remote_copy(
                src_ref=sends.at[k, a * n_sub + b],
                dst_ref=recvs.at[k, me],
                send_sem=ssem.at[k],
                recv_sem=rsem.at[k],
                device_id=(a, b),
                device_id_type=MESH,
            ).start()

        with scope(f"ex{k}"):
            each(one, True)
            pltpu.make_async_copy(sends.at[k, me], recvs.at[k, me], loc_sem.at[k]).start()

    def arrive(k):
        with scope(f"arr{k}"):
            pltpu.make_async_copy(sends.at[k, me], recvs.at[k, me], loc_sem.at[k]).wait()
            all_in = recvs.at[k, pl.ds(0, n_dev - 1)]
            pltpu.make_async_copy(all_in, all_in, rsem.at[k]).wait()
        return recvs[k].reshape(n_mir, dim)

    def sent(k):
        all_out = sends.at[k, pl.ds(0, n_dev - 1)]
        pltpu.make_async_copy(all_out, all_out, ssem.at[k]).wait()

    def rows(ref, i):
        return ref.at[pl.ds(pl.multiple_of(i * blk, blk), blk), :]

    def fill(k, value):
        sends[k] = value.astype(BF16).reshape(n_dev, per_peer, dim)

    with scope("prep"):
        loads[0].wait()
        loads[1].wait()
        lists = send_ref[...]
        parts = jnp.concatenate([lists // 32, lists % 32], axis=0).astype(F32).astype(BF16)
        lane = lax.broadcasted_iota(jnp.int32, (n_dev, n_mir), 1)
        widen = (
            lax.shift_right_logical(lane, 2) == lax.broadcasted_iota(jnp.int32, (n_dev, n_mir), 0)
        ).astype(BF16)
        wide = nn(parts, widen)
        wide = wide[:per_peer] * 32.0 + wide[per_peer:]
        turn_of = lax.broadcasted_iota(jnp.int32, (per_peer, n_mir), 1) & 3
        mine_of = turn_of == lax.broadcasted_iota(jnp.int32, (per_peer, n_mir), 0)
        picked = jnp.sum(jnp.where(mine_of, wide, 0.0), axis=0, keepdims=True).astype(jnp.int32)
        place[...] = (lax.broadcasted_iota(jnp.int32, (nodes, n_mir), 0) == picked).astype(BF16)
        inv_row = 1.0 / jnp.maximum(in_count_ref[...], 1).astype(F32)
        inv_col = jnp.broadcast_to(inv_row, (128, nodes)).T
        inv[...] = jnp.concatenate([inv_col] * (dim // 128), axis=1)
        loads[6].wait()
        fill(0, tn(place[...], feat[...]))
        loads[7].wait()
        ybuf[...] = (cot[...].astype(F32) * inv[...]).astype(BF16)
        fill(1, tn(place[...], ybuf[...]))

    with scope("hot"):
        for c in loads[2:6]:
            c.wait()
        edges = src_ref.shape[1]
        live = lax.broadcasted_iota(jnp.int32, (1, edges), 1) < count_ref[...]
        src_row = jnp.where(live, src_ref[...], -1)
        dst_row = jnp.where(live, dst_ref[...], -1)

        def hot(i, _):
            ids = lax.broadcasted_iota(jnp.int32, (blk, edges), 0) + i * blk
            rows(src_hot, i)[...] = (ids == src_row).astype(ONE_HOT)
            rows(dst_hot, i)[...] = (ids == dst_row).astype(ONE_HOT)
            return 0

        lax.fori_loop(0, slots // blk, hot, 0)

    with scope("bwait"):
        pl.semaphore_wait(barrier, n_dev - 1)
    exchange(0)
    exchange(1)

    with scope("build"):

        def build(i, _):
            rows(adj, i)[...] = nt(rows(dst_hot, i)[...], src_hot[...]).astype(BF16)
            return 0

        lax.fori_loop(0, slots // blk, build, 0)

    with scope("own1"):
        fown[...] = nn(adj[:, :nodes], feat[...])
        gown[...] = tn(adj[:nodes, :], ybuf[...])
        for c in loads[8:]:
            c.wait()

    fm = arrive(0)
    fill(2, fown[nodes:, :] + nn(adj[nodes:, nodes:], fm))
    exchange(2)
    gm = arrive(1)
    fill(3, gown[nodes:, :] + tn(adj[nodes:, nodes:], gm))
    exchange(3)
    with scope("own2"):
        fown[:nodes, :] += nn(adj[:nodes, nodes:], fm)
        gown[:nodes, :] += tn(adj[nodes:, :nodes], gm)
        zbuf[...] = nn(feat[...], wts[0]) + bias_ref[...]
        gbuf[...] = nt(cot[...], wts[2])

    fm2 = arrive(2)
    with scope("dense1"):

        def dense_z(i, _):
            here = pl.ds(pl.multiple_of(i * blk, blk), blk)
            mean = ((fown[here, :] + nn(place[here, :], fm2)) * inv[here, :]).astype(BF16)
            mbuf[here, :] = mean
            z = zbuf[here, :] + nn(mean, wts[1])
            sig = 1.0 / (1.0 + jnp.exp(-z))
            hbuf[here, :] = (z * sig).astype(BF16)
            zbuf[here, :] = sig * (1.0 + z * (1.0 - sig))
            return 0

        lax.fori_loop(0, nodes // blk, dense_z, 0)
        wpart[pl.ds(2 * dim, dim), :] = tn(hbuf[...], cot[...])

    gm2 = arrive(3)
    with scope("dense2"):

        def dense_g(i, acc):
            here = pl.ds(pl.multiple_of(i * blk, blk), blk)
            gsum = (gown[here, :] + nn(place[here, :], gm2)).astype(BF16)
            gown[here, :] = gsum.astype(F32)
            gh = gbuf[here, :] + nt(gsum, wts[3])
            gz = (gh * zbuf[here, :]).astype(BF16)
            gzbuf[here, :] = gz
            gzf = gz.astype(F32)
            ybuf[here, :] = (gzf * inv[here, :]).astype(BF16)
            return acc + jnp.sum(gzf, axis=0, keepdims=True)

        bpart[...] = lax.fori_loop(0, nodes // blk, dense_g, jnp.zeros((1, dim), F32))

    with scope("pick3"):
        fill(4, tn(place[...], ybuf[...]))
    exchange(4)

    with scope("wgrad"):
        wpart[pl.ds(0, dim), :] = tn(feat[...], gzbuf[...])
        wpart[pl.ds(dim, dim), :] = tn(mbuf[...], gzbuf[...])
        wpart[pl.ds(3 * dim, dim), :] = tn(hbuf[...], gown[:nodes, :].astype(BF16))
    mine = pl.ds(pl.multiple_of(core * half, half), half)
    other = pl.ds(pl.multiple_of((1 - core) * half, half), half)
    pair_w = pltpu.make_async_remote_copy(
        src_ref=wpart.at[other, :],
        dst_ref=wpair,
        send_sem=ssem.at[6],
        recv_sem=rsem.at[6],
        device_id=partner,
        device_id_type=MESH,
    )
    pair_b = pltpu.make_async_remote_copy(
        src_ref=bpart,
        dst_ref=bpair,
        send_sem=ssem.at[7],
        recv_sem=rsem.at[7],
        device_id=partner,
        device_id_type=MESH,
    )
    pair_w.start()
    pair_b.start()

    with scope("own3"):
        hown[...] = tn(adj[:nodes, :], ybuf[...])

    with scope("pairwait"):
        pair_w.wait()
        pair_b.wait()
    rs_send[...] = (wpart[mine, :] + wpair[...]).astype(rs_send.dtype).reshape(rs_send.shape)
    bsum[...] = bpart[...] + bpair[...]

    def scatter(a, b):
        pltpu.make_async_remote_copy(
            src_ref=rs_send.at[lax.div(a * n_sub + b, 2)],
            dst_ref=rs_recv.at[chip],
            send_sem=ssem.at[8],
            recv_sem=rsem.at[8],
            device_id=(a, b),
            device_id_type=MESH,
        ).start()
        pltpu.make_async_remote_copy(
            src_ref=bsum,
            dst_ref=brecv.at[chip],
            send_sem=ssem.at[9],
            recv_sem=rsem.at[9],
            device_id=(a, b),
            device_id_type=MESH,
        ).start()

    with scope("scatter"):
        each(scatter, False)
        own_rs = pltpu.make_async_copy(rs_send.at[chip], rs_recv.at[chip], loc_sem.at[6])
        own_rs.start()
        own_b = pltpu.make_async_copy(bsum, brecv.at[chip], loc_sem.at[7])
        own_b.start()

    hm = arrive(4)
    fill(5, hown[nodes:, :] + tn(adj[nodes:, nodes:], hm))
    exchange(5)
    with scope("own4"):
        hown[:nodes, :] += tn(adj[nodes:, :nodes], hm)
        zbuf[...] = nt(gzbuf[...], wts[0])

    with scope("rswait"):
        own_rs.wait()
        own_b.wait()
        others = rs_recv.at[pl.ds(0, n_chip - 1)]
        pltpu.make_async_copy(others, others, rsem.at[8]).wait()
        others = brecv.at[pl.ds(0, n_chip - 1)]
        pltpu.make_async_copy(others, others, rsem.at[9]).wait()
    ag_send[...] = (jnp.sum(rs_recv[...].astype(F32), axis=0) * norm_factor).astype(ag_send.dtype)
    gb_ref[...] = jnp.sum(brecv[...], axis=0) * norm_factor

    def gather(a, b):
        pltpu.make_async_remote_copy(
            src_ref=ag_send,
            dst_ref=ag_all.at[core, chip],
            send_sem=ssem.at[10],
            recv_sem=rsem.at[10],
            device_id=(a, b),
            device_id_type=MESH,
        ).start()

    with scope("gather"):
        each(gather, False)
        own_ag = pltpu.make_async_copy(ag_send, ag_all.at[core, chip], loc_sem.at[8])
        own_ag.start()

    hm2 = arrive(5)
    with scope("last"):

        def last(i, _):
            here = pl.ds(pl.multiple_of(i * blk, blk), blk)
            hsum = (hown[here, :] + nn(place[here, :], hm2)).astype(BF16)
            gfeat_ref[here, :] = (zbuf[here, :] + nt(hsum, wts[1])).astype(BF16)
            return 0

        lax.fori_loop(0, nodes // blk, last, 0)

    with scope("agwait"):
        own_ag.wait()
        others = ag_all.at[core, pl.ds(0, n_chip - 1)]
        pltpu.make_async_copy(others, others, rsem.at[10]).wait()
    swap = pltpu.make_async_remote_copy(
        src_ref=ag_all.at[core],
        dst_ref=ag_all.at[core],
        send_sem=ssem.at[11],
        recv_sem=rsem.at[11],
        device_id=partner,
        device_id_type=MESH,
    )
    with scope("swap"):
        swap.start()
        swap.wait()
    gw_ref[...] = ag_all[...].astype(F32).reshape(4 * dim, dim)

    with scope("drain"):
        for k in range(6):
            sent(k)
        for ref, k in ((rs_send, 8), (brecv, 9)):
            others = ref.at[pl.ds(0, n_chip - 1)]
            pltpu.make_async_copy(others, others, ssem.at[k]).wait()
        others = ag_all.at[core, pl.ds(0, n_chip - 1)]
        pltpu.make_async_copy(others, others, ssem.at[10]).wait()


def shards(
    n_dom,
    n_sub,
    features,
    cotangent,
    w_self_one,
    w_nbr_one,
    bias_one,
    w_self_two,
    w_nbr_two,
    in_count,
    send_list,
    src_slot,
    dst_slot,
    edge_count,
):
    nodes, dim = features.shape
    n_dev = n_dom * n_sub
    n_chip = n_dev // 2
    per_peer = send_list.shape[2]
    n_mir = n_dev * per_peer
    slots = nodes + n_mir
    edges = src_slot.shape[1]
    own_rows = 2 * dim // n_chip
    vm = pl.BlockSpec(memory_space=pltpu.VMEM)
    hbm = pl.BlockSpec(memory_space=pltpu.HBM)
    norm_factor = float(nodes * n_dev) ** -0.5
    full = pltpu.VMEM((nodes, dim), F32)
    fullb = pltpu.VMEM((nodes, dim), BF16)
    allf = pltpu.VMEM((slots, dim), F32)
    msgs = pltpu.VMEM((6, n_dev, per_peer, dim), BF16)
    rs_t = BF16
    ag_t = BF16
    gfeat, gw, gb = pl.pallas_call(
        functools.partial(kernel, n_dom, n_sub, norm_factor),
        out_shape=(
            jax.ShapeDtypeStruct((nodes, dim), BF16),
            jax.ShapeDtypeStruct((4 * dim, dim), F32),
            jax.ShapeDtypeStruct((1, dim), F32),
        ),
        in_specs=[hbm] * 12,
        out_specs=(vm, vm, vm),
        scratch_shapes=[
            pltpu.VMEM((1, 1), jnp.int32),
            pltpu.VMEM((1, edges), jnp.int32),
            pltpu.VMEM((1, edges), jnp.int32),
            pltpu.VMEM((per_peer, n_dev), jnp.int32),
            pltpu.VMEM((1, nodes), jnp.int32),
            pltpu.VMEM((1, dim), F32),
            fullb,
            fullb,
            pltpu.VMEM((4, dim, dim), BF16),
            pltpu.VMEM((slots, edges), ONE_HOT),
            pltpu.VMEM((slots, edges), ONE_HOT),
            pltpu.VMEM((slots, slots), BF16),
            pltpu.VMEM((nodes, n_mir), BF16),
            full,
            fullb,
            full,
            full,
            allf,
            allf,
            allf,
            fullb,
            fullb,
            fullb,
            msgs,
            msgs,
            pltpu.VMEM((4 * dim, dim), F32),
            pltpu.VMEM((1, dim), F32),
            pltpu.VMEM((2 * dim, dim), F32),
            pltpu.VMEM((1, dim), F32),
            pltpu.VMEM((1, dim), F32),
            pltpu.VMEM((n_chip, 1, dim), F32),
            pltpu.VMEM((n_chip, own_rows, dim), rs_t),
            pltpu.VMEM((n_chip, own_rows, dim), rs_t),
            pltpu.VMEM((own_rows, dim), ag_t),
            pltpu.VMEM((2, n_chip, own_rows, dim), ag_t),
            pltpu.SemaphoreType.DMA((12,)),
            pltpu.SemaphoreType.DMA((9,)),
            pltpu.SemaphoreType.DMA((12,)),
            pltpu.SemaphoreType.DMA((12,)),
        ],
        compiler_params=pltpu.CompilerParams(
            collective_id=0, has_side_effects=True, vmem_limit_bytes=44 << 20
        ),
    )(
        edge_count.reshape(1, 1),
        *(
            pltpu.with_memory_space_constraint(x, pltpu.HBM)
            for x in (
                src_slot,
                dst_slot,
                send_list[0].T,
                in_count.reshape(1, nodes),
                bias_one.reshape(1, dim),
                features,
                cotangent,
                w_self_one,
                w_nbr_one,
                w_self_two,
                w_nbr_two,
            )
        ),
    )
    return gfeat, gw.reshape(4, dim, dim), gb.reshape(dim)


def solution(mesh):
    both = ("dom", "sub")
    return jax.shard_map(
        functools.partial(shards, mesh.shape["dom"], mesh.shape["sub"]),
        mesh=mesh,
        in_specs=(
            P(both, None),
            P(both, None),
            P(),
            P(),
            P(),
            P(),
            P(),
            P(both),
            P(both, None, None),
            P(both, None),
            P(both, None),
            P(both),
        ),
        out_specs=(P(both, None), P(), P()),
        check_vma=False,
    )
```

time: 67.2 us -> 57 us (0.85)
  Pallas kernels: 60.7 us -> 53.2 us
  local copies, waits for them, and re-layouts: 4.97 us -> 2.33 us
    pallas_call x1, Pallas kernels: 60.7 us -> 53.2 us  [shards(): pl.pallas_call(functools.partial(kernel, n_dom, n_sub, norm_factor), out_...]
    unnamed x10 -> x3, local copies, waits for them, and re-layouts: 4.28 us -> 2.33 us
    reshape x1 -> x0, local copies, waits for them, and re-layouts: 0.69 us -> none  [shards(): send_list.reshape(1, n_mir)]
where the time goes in v2:
time: 57 us; the launch traced here: 56.9 us
  Pallas kernels  53.2 us (93%)
  local copies, waits for them, and re-layouts  2.33 us (4%)
  between operations  1.29 us (2%)
    pallas_call x1, Pallas kernels, shards(): pl.pallas_call(functools.partial(kernel, n_dom, n_sub, norm_factor), out_...  53.2 us
    unnamed x3, local copies, waits for them, and re-layouts  2.33 us

profile of v2, /device:TPU:1, one launch (start us, length us, event | category | flops | bytes accessed | tf_op | source)
XLA Modules:
  0.0 56.9 jit_solution(18080553001184167205)
XLA Ops:
  1.3 53.2 %shard_map.139 = (bf16[1024,256]{1,0:T(8,128)(2,1)S(1)}, f32[1024,256]{1,0:T(8,128)S(1)}, f32[1,256]{1,0:T(1,128)S(1)}) custom-call(s32[1,1]{1,0:T(1,128)} %bitcast.8.count_hbm, s32[1,2048]{1,0:T(1,128)} %src_hbm.1, s32[1,2048]{1,0:T(1,128)} %dst_hbm.1, s32[4,128]{1,0:T(4,128)} %bitcast.12, s32[1,1024]{1,0:T(1,128)} %bitcast.11, f32[1,256]{1,0:T(1,128)} %bitcast.13, ...), custom_call_target="tpu_custom_call" | custom-call | tf_op jit(solution)/shard_map/pallas_call | solution.py:472
  54.5 0.8 %copy.19 = bf16[1024,256]{1,0:T(8,128)(2,1)} copy(bf16[1024,256]{1,0:T(8,128)(2,1)S(1)} %get-tuple-element.12) | data formatting | bytes 1048576
  55.3 1.0 %copy.20 = f32[4,256,256]{2,1,0:T(8,128)} copy(f32[4,256,256]{2,1,0:T(8,128)S(1)} %bitcast.9) | data formatting | bytes 2097152
  56.3 0.6 copy.21

commit v3 on v2

--- a/solution.py
+++ b/solution.py
@@ -84,6 +84,7 @@
     mbuf,
     hbuf,
     gzbuf,
+    gsbuf,
     sends,
     recvs,
     wpart,
@@ -200,9 +201,14 @@
     def fill(k, value):
         sends[k] = value.astype(BF16).reshape(n_dev, per_peer, dim)
 
-    with scope("prep"):
+    def hot_block(index_row, i):
+        shape = (blk, index_row.shape[1])
+        ids = lax.broadcasted_iota(jnp.int32, shape, 0).astype(F32).astype(BF16)
+        here = (index_row - i * blk).astype(F32).astype(BF16)
+        return jnp.where(ids == here, jnp.ones(shape, BF16), jnp.zeros(shape, BF16))
+
+    with scope("prepf"):
         loads[0].wait()
-        loads[1].wait()
         lists = send_ref[...]
         parts = jnp.concatenate([lists // 32, lists % 32], axis=0).astype(F32).astype(BF16)
         lane = lax.broadcasted_iota(jnp.int32, (n_dev, n_mir), 1)
@@ -214,15 +220,24 @@
         turn_of = lax.broadcasted_iota(jnp.int32, (per_peer, n_mir), 1) & 3
         mine_of = turn_of == lax.broadcasted_iota(jnp.int32, (per_peer, n_mir), 0)
         picked = jnp.sum(jnp.where(mine_of, wide, 0.0), axis=0, keepdims=True).astype(jnp.int32)
-        place[...] = (lax.broadcasted_iota(jnp.int32, (nodes, n_mir), 0) == picked).astype(BF16)
+        for i in range(nodes // blk):
+            place[pl.ds(i * blk, blk), :] = hot_block(picked, i)
+        loads[6].wait()
+        fill(0, tn(place[...], feat[...]))
+
+    with scope("bwait"):
+        pl.semaphore_wait(barrier, n_dev - 1)
+    exchange(0)
+
+    with scope("prepg"):
+        loads[1].wait()
         inv_row = 1.0 / jnp.maximum(in_count_ref[...], 1).astype(F32)
         inv_col = jnp.broadcast_to(inv_row, (128, nodes)).T
         inv[...] = jnp.concatenate([inv_col] * (dim // 128), axis=1)
-        loads[6].wait()
-        fill(0, tn(place[...], feat[...]))
         loads[7].wait()
         ybuf[...] = (cot[...].astype(F32) * inv[...]).astype(BF16)
         fill(1, tn(place[...], ybuf[...]))
+    exchange(1)
 
     with scope("hot"):
         for c in loads[2:6]:
@@ -233,31 +248,35 @@
         dst_row = jnp.where(live, dst_ref[...], -1)
 
         def hot(i, _):
-            ids = lax.broadcasted_iota(jnp.int32, (blk, edges), 0) + i * blk
-            rows(src_hot, i)[...] = (ids == src_row).astype(ONE_HOT)
-            rows(dst_hot, i)[...] = (ids == dst_row).astype(ONE_HOT)
+            rows(src_hot, i)[...] = hot_block(src_row, i).astype(ONE_HOT)
+            rows(dst_hot, i)[...] = hot_block(dst_row, i).astype(ONE_HOT)
             return 0
 
         lax.fori_loop(0, slots // blk, hot, 0)
 
-    with scope("bwait"):
-        pl.semaphore_wait(barrier, n_dev - 1)
-    exchange(0)
-    exchange(1)
-
-    with scope("build"):
-
-        def build(i, _):
+    masters = nodes // blk
+    with scope("buildm"):
+
+        def build_rows(i, _):
             rows(adj, i)[...] = nt(rows(dst_hot, i)[...], src_hot[...]).astype(BF16)
             return 0
 
-        lax.fori_loop(0, slots // blk, build, 0)
+        lax.fori_loop(masters, slots // blk, build_rows, 0)
+
+        def build_columns(i, _):
+            here = pl.ds(pl.multiple_of(i * blk, blk), blk)
+            adj[here, nodes:] = nt(dst_hot[here, :], src_hot[nodes:, :]).astype(BF16)
+            return 0
+
+        lax.fori_loop(0, masters, build_columns, 0)
 
     with scope("own1"):
-        fown[...] = nn(adj[:, :nodes], feat[...])
-        gown[...] = tn(adj[:nodes, :], ybuf[...])
+        fown[nodes:, :] = nn(adj[nodes:, :nodes], feat[...])
+        gown[nodes:, :] = tn(adj[:nodes, nodes:], ybuf[...])
         for c in loads[8:]:
             c.wait()
+        zbuf[...] = nn(feat[...], wts[0]) + bias_ref[...]
+        gbuf[...] = nt(cot[...], wts[2])
 
     fm = arrive(0)
     fill(2, fown[nodes:, :] + nn(adj[nodes:, nodes:], fm))
@@ -265,52 +284,51 @@
     gm = arrive(1)
     fill(3, gown[nodes:, :] + tn(adj[nodes:, nodes:], gm))
     exchange(3)
+
+    with scope("buildo"):
+
+        def build_rest(i, _):
+            here = pl.ds(pl.multiple_of(i * blk, blk), blk)
+            adj[here, :nodes] = nt(dst_hot[here, :], src_hot[:nodes, :]).astype(BF16)
+            return 0
+
+        lax.fori_loop(0, masters, build_rest, 0)
     with scope("own2"):
-        fown[:nodes, :] += nn(adj[:nodes, nodes:], fm)
-        gown[:nodes, :] += tn(adj[nodes:, :nodes], gm)
-        zbuf[...] = nn(feat[...], wts[0]) + bias_ref[...]
-        gbuf[...] = nt(cot[...], wts[2])
-
+        fown[:nodes, :] = nn(adj[:nodes, :nodes], feat[...]) + nn(adj[:nodes, nodes:], fm)
+        gown[:nodes, :] = tn(adj[:nodes, :nodes], ybuf[...]) + tn(adj[nodes:, :nodes], gm)
+
+    big = nodes // 2
     fm2 = arrive(2)
     with scope("dense1"):
-
-        def dense_z(i, _):
-            here = pl.ds(pl.multiple_of(i * blk, blk), blk)
+        for i in range(nodes // big):
+            here = pl.ds(i * big, big)
             mean = ((fown[here, :] + nn(place[here, :], fm2)) * inv[here, :]).astype(BF16)
             mbuf[here, :] = mean
             z = zbuf[here, :] + nn(mean, wts[1])
             sig = 1.0 / (1.0 + jnp.exp(-z))
             hbuf[here, :] = (z * sig).astype(BF16)
             zbuf[here, :] = sig * (1.0 + z * (1.0 - sig))
-            return 0
-
-        lax.fori_loop(0, nodes // blk, dense_z, 0)
         wpart[pl.ds(2 * dim, dim), :] = tn(hbuf[...], cot[...])
 
     gm2 = arrive(3)
     with scope("dense2"):
-
-        def dense_g(i, acc):
-            here = pl.ds(pl.multiple_of(i * blk, blk), blk)
+        bias_sum = jnp.zeros((1, dim), F32)
+        for i in range(nodes // big):
+            here = pl.ds(i * big, big)
             gsum = (gown[here, :] + nn(place[here, :], gm2)).astype(BF16)
-            gown[here, :] = gsum.astype(F32)
+            gsbuf[here, :] = gsum
             gh = gbuf[here, :] + nt(gsum, wts[3])
             gz = (gh * zbuf[here, :]).astype(BF16)
             gzbuf[here, :] = gz
             gzf = gz.astype(F32)
             ybuf[here, :] = (gzf * inv[here, :]).astype(BF16)
-            return acc + jnp.sum(gzf, axis=0, keepdims=True)
-
-        bpart[...] = lax.fori_loop(0, nodes // blk, dense_g, jnp.zeros((1, dim), F32))
-
-    with scope("pick3"):
-        fill(4, tn(place[...], ybuf[...]))
-    exchange(4)
+            bias_sum += jnp.sum(gzf, axis=0, keepdims=True)
+        bpart[...] = bias_sum
 
     with scope("wgrad"):
         wpart[pl.ds(0, dim), :] = tn(feat[...], gzbuf[...])
         wpart[pl.ds(dim, dim), :] = tn(mbuf[...], gzbuf[...])
-        wpart[pl.ds(3 * dim, dim), :] = tn(hbuf[...], gown[:nodes, :].astype(BF16))
+        wpart[pl.ds(3 * dim, dim), :] = tn(hbuf[...], gsbuf[...])
     mine = pl.ds(pl.multiple_of(core * half, half), half)
     other = pl.ds(pl.multiple_of((1 - core) * half, half), half)
     pair_w = pltpu.make_async_remote_copy(
@@ -332,6 +350,10 @@
     pair_w.start()
     pair_b.start()
 
+    with scope("pick3"):
+        fill(4, tn(place[...], ybuf[...]))
+    exchange(4)
+
     with scope("own3"):
         hown[...] = tn(adj[:nodes, :], ybuf[...])
 
@@ -401,13 +423,10 @@
     hm2 = arrive(5)
     with scope("last"):
 
-        def last(i, _):
-            here = pl.ds(pl.multiple_of(i * blk, blk), blk)
+        for i in range(nodes // big):
+            here = pl.ds(i * big, big)
             hsum = (hown[here, :] + nn(place[here, :], hm2)).astype(BF16)
             gfeat_ref[here, :] = (zbuf[here, :] + nt(hsum, wts[1])).astype(BF16)
-            return 0
-
-        lax.fori_loop(0, nodes // blk, last, 0)
 
     with scope("agwait"):
         own_ag.wait()
@@ -434,6 +453,19 @@
             pltpu.make_async_copy(others, others, ssem.at[k]).wait()
         others = ag_all.at[core, pl.ds(0, n_chip - 1)]
         pltpu.make_async_copy(others, others, ssem.at[10]).wait()
+
+
+def put(*refs):
+    sem = refs[-1]
+    half = len(refs) // 2
+    copies = [
+        pltpu.make_async_copy(a, b, sem.at[i])
+        for i, (a, b) in enumerate(zip(refs[:half], refs[half:-1]))
+    ]
+    for c in copies:
+        c.start()
+    for c in copies:
+        c.wait()
 
 
 def shards(
@@ -502,6 +534,7 @@
             fullb,
             fullb,
             fullb,
+            fullb,
             msgs,
             msgs,
             pltpu.VMEM((4 * dim, dim), F32),
@@ -541,6 +574,15 @@
             )
         ),
     )
+    results = (gfeat, gw, gb)
+    gfeat, gw, gb = pl.pallas_call(
+        put,
+        out_shape=tuple(jax.ShapeDtypeStruct(x.shape, x.dtype) for x in results),
+        in_specs=[vm] * 3,
+        out_specs=(hbm,) * 3,
+        scratch_shapes=[pltpu.SemaphoreType.DMA((3,))],
+        compiler_params=pltpu.CompilerParams(vmem_limit_bytes=1 << 20),
+    )(*results)
     return gfeat, gw.reshape(4, dim, dim), gb.reshape(dim)
 
 

time: 57 us -> 53 us (0.930)
  local copies, waits for them, and re-layouts: 2.33 us -> 0 us
  Pallas kernels: 53.2 us -> 51.6 us
    pallas_call x1, Pallas kernels: 53.2 us -> 50.4 us  [shards(): pl.pallas_call(functools.partial(kernel, n_dom, n_sub, norm_factor), out_...]
    unnamed x3 -> x0, local copies, waits for them, and re-layouts: 2.33 us -> none
    pallas_call x0 -> x1, Pallas kernels: none -> 1.17 us  [shards(): pl.pallas_call(put, out_shape=tuple((jax.ShapeDtypeStruct(x.shape, x.dtyp...]
where the time goes in v3:
time: 53 us; the launch traced here: 52.9 us
  Pallas kernels  51.6 us (97%)
  between operations  1.29 us (2%)
    pallas_call x1, Pallas kernels, shards(): pl.pallas_call(functools.partial(kernel, n_dom, n_sub, norm_factor), out_...  50.4 us
    pallas_call x1, Pallas kernels, shards(): pl.pallas_call(put, out_shape=tuple((jax.ShapeDtypeStruct(x.shape, x.dtyp...  1.17 us

profile of v3, /device:TPU:1, one launch (start us, length us, event | category | flops | bytes accessed | tf_op | source)
XLA Modules:
  0.0 52.9 jit_solution(2463191887860599603)
XLA Ops:
  1.3 50.4 %shard_map.139 = (bf16[1024,256]{1,0:T(8,128)(2,1)S(1)}, f32[1024,256]{1,0:T(8,128)S(1)}, f32[1,256]{1,0:T(1,128)S(1)}) custom-call(s32[1,1]{1,0:T(1,128)} %bitcast.8.count_hbm, s32[1,2048]{1,0:T(1,128)} %src_hbm.1, s32[1,2048]{1,0:T(1,128)} %dst_hbm.1, s32[4,128]{1,0:T(4,128)} %bitcast.10, s32[1,1024]{1,0:T(1,128)} %bitcast.9, f32[1,256]{1,0:T(1,128)} %bitcast.11, ...), custom_call_target="tpu_custom_call" | custom-call | tf_op jit(solution)/shard_map/pallas_call | solution.py:504
  51.7 1.2 %shard_map.140 = (bf16[1024,256]{1,0:T(8,128)(2,1)}, f32[1024,256]{1,0:T(8,128)}, f32[1,256]{1,0:T(1,128)}) custom-call(bf16[1024,256]{1,0:T(8,128)(2,1)S(1)} %get-tuple-element.9.refs_0_, f32[1024,256]{1,0:T(8,128)S(1)} %get-tuple-element.10.refs_1_, f32[1,256]{1,0:T(1,128)S(1)} %get-tuple-element.11.refs_2_), custom_call_target="tpu_custom_call" | custom-call | tf_op jit(solution)/shard_map/pallas_call | solution.py:578

commit v4 on v3

--- a/solution.py
+++ b/solution.py
@@ -74,6 +74,7 @@
     dst_hot,
     adj,
     place,
+    picks,
     inv,
     ybuf,
     zbuf,
@@ -89,6 +90,7 @@
     recvs,
     wpart,
     bpart,
+    wsend,
     wpair,
     bpair,
     bsum,
@@ -222,8 +224,24 @@
         picked = jnp.sum(jnp.where(mine_of, wide, 0.0), axis=0, keepdims=True).astype(jnp.int32)
         for i in range(nodes // blk):
             place[pl.ds(i * blk, blk), :] = hot_block(picked, i)
+        picks[...] = place[...].T
         loads[6].wait()
-        fill(0, tn(place[...], feat[...]))
+        fill(0, nn(picks[...], feat[...]))
+
+    with scope("hot"):
+        for c in loads[2:6]:
+            c.wait()
+        edges = src_ref.shape[1]
+        live = lax.broadcasted_iota(jnp.int32, (1, edges), 1) < count_ref[...]
+        src_row = jnp.where(live, src_ref[...], -1)
+        dst_row = jnp.where(live, dst_ref[...], -1)
+
+        def hot(i, _):
+            rows(src_hot, i)[...] = hot_block(src_row, i).astype(ONE_HOT)
+            rows(dst_hot, i)[...] = hot_block(dst_row, i).astype(ONE_HOT)
+            return 0
+
+        lax.fori_loop(0, slots // blk, hot, 0)
 
     with scope("bwait"):
         pl.semaphore_wait(barrier, n_dev - 1)
@@ -236,23 +254,8 @@
         inv[...] = jnp.concatenate([inv_col] * (dim // 128), axis=1)
         loads[7].wait()
         ybuf[...] = (cot[...].astype(F32) * inv[...]).astype(BF16)
-        fill(1, tn(place[...], ybuf[...]))
+        fill(1, nn(picks[...], ybuf[...]))
     exchange(1)
-
-    with scope("hot"):
-        for c in loads[2:6]:
-            c.wait()
-        edges = src_ref.shape[1]
-        live = lax.broadcasted_iota(jnp.int32, (1, edges), 1) < count_ref[...]
-        src_row = jnp.where(live, src_ref[...], -1)
-        dst_row = jnp.where(live, dst_ref[...], -1)
-
-        def hot(i, _):
-            rows(src_hot, i)[...] = hot_block(src_row, i).astype(ONE_HOT)
-            rows(dst_hot, i)[...] = hot_block(dst_row, i).astype(ONE_HOT)
-            return 0
-
-        lax.fori_loop(0, slots // blk, hot, 0)
 
     masters = nodes // blk
     with scope("buildm"):
@@ -325,14 +328,19 @@
             bias_sum += jnp.sum(gzf, axis=0, keepdims=True)
         bpart[...] = bias_sum
 
+    with scope("pick3"):
+        fill(4, nn(picks[...], ybuf[...]))
+    exchange(4)
+
     with scope("wgrad"):
         wpart[pl.ds(0, dim), :] = tn(feat[...], gzbuf[...])
         wpart[pl.ds(dim, dim), :] = tn(mbuf[...], gzbuf[...])
         wpart[pl.ds(3 * dim, dim), :] = tn(hbuf[...], gsbuf[...])
     mine = pl.ds(pl.multiple_of(core * half, half), half)
     other = pl.ds(pl.multiple_of((1 - core) * half, half), half)
+    wsend[...] = wpart[other, :].astype(BF16)
     pair_w = pltpu.make_async_remote_copy(
-        src_ref=wpart.at[other, :],
+        src_ref=wsend,
         dst_ref=wpair,
         send_sem=ssem.at[6],
         recv_sem=rsem.at[6],
@@ -350,17 +358,13 @@
     pair_w.start()
     pair_b.start()
 
-    with scope("pick3"):
-        fill(4, tn(place[...], ybuf[...]))
-    exchange(4)
-
     with scope("own3"):
         hown[...] = tn(adj[:nodes, :], ybuf[...])
 
     with scope("pairwait"):
         pair_w.wait()
         pair_b.wait()
-    rs_send[...] = (wpart[mine, :] + wpair[...]).astype(rs_send.dtype).reshape(rs_send.shape)
+    rs_send[...] = (wpart[mine, :] + wpair[...].astype(F32)).astype(rs_send.dtype).reshape(rs_send.shape)
     bsum[...] = bpart[...] + bpair[...]
 
     def scatter(a, b):
@@ -372,6 +376,20 @@
             device_id=(a, b),
             device_id_type=MESH,
         ).start()
+
+    with scope("scatter"):
+        each(scatter, False)
+        own_rs = pltpu.make_async_copy(rs_send.at[chip], rs_recv.at[chip], loc_sem.at[6])
+        own_rs.start()
+
+    hm = arrive(4)
+    fill(5, hown[nodes:, :] + tn(adj[nodes:, nodes:], hm))
+    exchange(5)
+    with scope("own4"):
+        hown[:nodes, :] += tn(adj[nodes:, :nodes], hm)
+        zbuf[...] = nt(gzbuf[...], wts[0])
+
+    def spread_bias(a, b):
         pltpu.make_async_remote_copy(
             src_ref=bsum,
             dst_ref=brecv.at[chip],
@@ -381,29 +399,16 @@
             device_id_type=MESH,
         ).start()
 
-    with scope("scatter"):
-        each(scatter, False)
-        own_rs = pltpu.make_async_copy(rs_send.at[chip], rs_recv.at[chip], loc_sem.at[6])
-        own_rs.start()
+    with scope("bias"):
+        each(spread_bias, False)
         own_b = pltpu.make_async_copy(bsum, brecv.at[chip], loc_sem.at[7])
         own_b.start()
 
-    hm = arrive(4)
-    fill(5, hown[nodes:, :] + tn(adj[nodes:, nodes:], hm))
-    exchange(5)
-    with scope("own4"):
-        hown[:nodes, :] += tn(adj[nodes:, :nodes], hm)
-        zbuf[...] = nt(gzbuf[...], wts[0])
-
     with scope("rswait"):
         own_rs.wait()
-        own_b.wait()
         others = rs_recv.at[pl.ds(0, n_chip - 1)]
         pltpu.make_async_copy(others, others, rsem.at[8]).wait()
-        others = brecv.at[pl.ds(0, n_chip - 1)]
-        pltpu.make_async_copy(others, others, rsem.at[9]).wait()
     ag_send[...] = (jnp.sum(rs_recv[...].astype(F32), axis=0) * norm_factor).astype(ag_send.dtype)
-    gb_ref[...] = jnp.sum(brecv[...], axis=0) * norm_factor
 
     def gather(a, b):
         pltpu.make_async_remote_copy(
@@ -432,6 +437,10 @@
         own_ag.wait()
         others = ag_all.at[core, pl.ds(0, n_chip - 1)]
         pltpu.make_async_copy(others, others, rsem.at[10]).wait()
+    own_b.wait()
+    others = brecv.at[pl.ds(0, n_chip - 1)]
+    pltpu.make_async_copy(others, others, rsem.at[9]).wait()
+    gb_ref[...] = jnp.sum(brecv[...], axis=0) * norm_factor
     swap = pltpu.make_async_remote_copy(
         src_ref=ag_all.at[core],
         dst_ref=ag_all.at[core],
@@ -524,6 +533,7 @@
             pltpu.VMEM((slots, edges), ONE_HOT),
             pltpu.VMEM((slots, slots), BF16),
             pltpu.VMEM((nodes, n_mir), BF16),
+            pltpu.VMEM((n_mir, nodes), BF16),
             full,
             fullb,
             full,
@@ -539,7 +549,8 @@
             msgs,
             pltpu.VMEM((4 * dim, dim), F32),
             pltpu.VMEM((1, dim), F32),
-            pltpu.VMEM((2 * dim, dim), F32),
+            pltpu.VMEM((2 * dim, dim), BF16),
+            pltpu.VMEM((2 * dim, dim), BF16),
             pltpu.VMEM((1, dim), F32),
             pltpu.VMEM((1, dim), F32),
             pltpu.VMEM((n_chip, 1, dim), F32),

time: 53 us -> 51.3 us (0.968)
  Pallas kernels: 51.6 us -> 49.9 us
    pallas_call x1, Pallas kernels: 50.4 us -> 48.7 us  [shards(): pl.pallas_call(functools.partial(kernel, n_dom, n_sub, norm_factor), out_...]
where the time goes in v4:
time: 51.3 us; the launch traced here: 51.2 us
  Pallas kernels  49.9 us (97%)
  between operations  1.29 us (3%)
    pallas_call x1, Pallas kernels, shards(): pl.pallas_call(functools.partial(kernel, n_dom, n_sub, norm_factor), out_...  48.7 us
    pallas_call x1, Pallas kernels, shards(): pl.pallas_call(put, out_shape=tuple((jax.ShapeDtypeStruct(x.shape, x.dtyp...  1.17 us

profile of v4, /device:TPU:1, one launch (start us, length us, event | category | flops | bytes accessed | tf_op | source)
XLA Modules:
  0.0 51.2 jit_solution(12458561838897831782)
XLA Ops:
  1.3 48.7 %shard_map.139 = (bf16[1024,256]{1,0:T(8,128)(2,1)S(1)}, f32[1024,256]{1,0:T(8,128)S(1)}, f32[1,256]{1,0:T(1,128)S(1)}) custom-call(s32[1,1]{1,0:T(1,128)} %bitcast.8.count_hbm, s32[1,2048]{1,0:T(1,128)} %src_hbm.1, s32[1,2048]{1,0:T(1,128)} %dst_hbm.1, s32[4,128]{1,0:T(4,128)} %bitcast.10, s32[1,1024]{1,0:T(1,128)} %bitcast.9, f32[1,256]{1,0:T(1,128)} %bitcast.11, ...), custom_call_target="tpu_custom_call" | custom-call | tf_op jit(solution)/shard_map/pallas_call | solution.py:513
  50.0 1.2 %shard_map.140 = (bf16[1024,256]{1,0:T(8,128)(2,1)}, f32[1024,256]{1,0:T(8,128)}, f32[1,256]{1,0:T(1,128)}) custom-call(bf16[1024,256]{1,0:T(8,128)(2,1)S(1)} %get-tuple-element.9.refs_0_, f32[1024,256]{1,0:T(8,128)S(1)} %get-tuple-element.10.refs_1_, f32[1,256]{1,0:T(1,128)S(1)} %get-tuple-element.11.refs_2_), custom_call_target="tpu_custom_call" | custom-call | tf_op jit(solution)/shard_map/pallas_call | solution.py:589

commit v5 on v4

--- a/solution.py
+++ b/solution.py
@@ -103,6 +103,7 @@
     loc_sem,
     ssem,
     rsem,
+    bsem,
 ):
     nodes, dim = feat.shape
     n_dev = n_dom * n_sub
@@ -365,7 +366,32 @@
         pair_w.wait()
         pair_b.wait()
     rs_send[...] = (wpart[mine, :] + wpair[...].astype(F32)).astype(rs_send.dtype).reshape(rs_send.shape)
-    bsum[...] = bpart[...] + bpair[...]
+    bias_pair = bpart[...] + bpair[...]
+
+    places = (at_x, at_z, at_y)
+
+    def bias_out(stage, value):
+        bsum[stage] = value
+        brecv[stage, places[stage]] = value
+        for k in (2, 1, 3):
+            to = (
+                (d, wrap4(at_x + k) * 2 + core),
+                (at_y * 4 + wrap4(at_z + k), s),
+                (wrap4(at_y + k) * 4 + at_z, s),
+            )[stage]
+            pltpu.make_async_remote_copy(
+                src_ref=bsum.at[stage],
+                dst_ref=brecv.at[stage, places[stage]],
+                send_sem=bsem.at[0, stage],
+                recv_sem=bsem.at[1, stage],
+                device_id=to,
+                device_id_type=MESH,
+            ).start()
+
+    def bias_in(stage):
+        others = brecv.at[stage, pl.ds(0, 3)]
+        pltpu.make_async_copy(others, others, bsem.at[1, stage]).wait()
+        return jnp.sum(brecv[stage], axis=0)
 
     def scatter(a, b):
         pltpu.make_async_remote_copy(
@@ -377,32 +403,19 @@
             device_id_type=MESH,
         ).start()
 
+    bias_out(0, bias_pair)
     with scope("scatter"):
         each(scatter, False)
         own_rs = pltpu.make_async_copy(rs_send.at[chip], rs_recv.at[chip], loc_sem.at[6])
         own_rs.start()
 
     hm = arrive(4)
+    bias_out(1, bias_in(0))
     fill(5, hown[nodes:, :] + tn(adj[nodes:, nodes:], hm))
     exchange(5)
     with scope("own4"):
         hown[:nodes, :] += tn(adj[nodes:, :nodes], hm)
         zbuf[...] = nt(gzbuf[...], wts[0])
-
-    def spread_bias(a, b):
-        pltpu.make_async_remote_copy(
-            src_ref=bsum,
-            dst_ref=brecv.at[chip],
-            send_sem=ssem.at[9],
-            recv_sem=rsem.at[9],
-            device_id=(a, b),
-            device_id_type=MESH,
-        ).start()
-
-    with scope("bias"):
-        each(spread_bias, False)
-        own_b = pltpu.make_async_copy(bsum, brecv.at[chip], loc_sem.at[7])
-        own_b.start()
 
     with scope("rswait"):
         own_rs.wait()
@@ -420,6 +433,7 @@
             device_id_type=MESH,
         ).start()
 
+    bias_out(2, bias_in(1))
     with scope("gather"):
         each(gather, False)
         own_ag = pltpu.make_async_copy(ag_send, ag_all.at[core, chip], loc_sem.at[8])
@@ -437,10 +451,6 @@
         own_ag.wait()
         others = ag_all.at[core, pl.ds(0, n_chip - 1)]
         pltpu.make_async_copy(others, others, rsem.at[10]).wait()
-    own_b.wait()
-    others = brecv.at[pl.ds(0, n_chip - 1)]
-    pltpu.make_async_copy(others, others, rsem.at[9]).wait()
-    gb_ref[...] = jnp.sum(brecv[...], axis=0) * norm_factor
     swap = pltpu.make_async_remote_copy(
         src_ref=ag_all.at[core],
         dst_ref=ag_all.at[core],
@@ -451,15 +461,18 @@
     )
     with scope("swap"):
         swap.start()
+        gb_ref[...] = bias_in(2) * norm_factor
         swap.wait()
     gw_ref[...] = ag_all[...].astype(F32).reshape(4 * dim, dim)
 
     with scope("drain"):
         for k in range(6):
             sent(k)
-        for ref, k in ((rs_send, 8), (brecv, 9)):
-            others = ref.at[pl.ds(0, n_chip - 1)]
-            pltpu.make_async_copy(others, others, ssem.at[k]).wait()
+        others = rs_send.at[pl.ds(0, n_chip - 1)]
+        pltpu.make_async_copy(others, others, ssem.at[8]).wait()
+        for stage in range(3):
+            others = brecv.at[stage, pl.ds(0, 3)]
+            pltpu.make_async_copy(others, others, bsem.at[0, stage]).wait()
         others = ag_all.at[core, pl.ds(0, n_chip - 1)]
         pltpu.make_async_copy(others, others, ssem.at[10]).wait()
 
@@ -552,8 +565,8 @@
             pltpu.VMEM((2 * dim, dim), BF16),
             pltpu.VMEM((2 * dim, dim), BF16),
             pltpu.VMEM((1, dim), F32),
-            pltpu.VMEM((1, dim), F32),
-            pltpu.VMEM((n_chip, 1, dim), F32),
+            pltpu.VMEM((3, 1, dim), F32),
+            pltpu.VMEM((3, 4, 1, dim), F32),
             pltpu.VMEM((n_chip, own_rows, dim), rs_t),
             pltpu.VMEM((n_chip, own_rows, dim), rs_t),
             pltpu.VMEM((own_rows, dim), ag_t),
@@ -562,6 +575,7 @@
             pltpu.SemaphoreType.DMA((9,)),
             pltpu.SemaphoreType.DMA((12,)),
             pltpu.SemaphoreType.DMA((12,)),
+            pltpu.SemaphoreType.DMA((2, 3)),
         ],
         compiler_params=pltpu.CompilerParams(
             collective_id=0, has_side_effects=True, vmem_limit_bytes=44 << 20

time: 51.3 us -> 50.7 us (0.988)
  Pallas kernels: 49.9 us -> 49.3 us
    pallas_call x1, Pallas kernels: 48.7 us -> 48.2 us  [shards(): pl.pallas_call(functools.partial(kernel, n_dom, n_sub, norm_factor), out_...]
where the time goes in v5:
time: 50.7 us; the launch traced here: 50.6 us
  Pallas kernels  49.3 us (97%)
  between operations  1.29 us (3%)
    pallas_call x1, Pallas kernels, shards(): pl.pallas_call(functools.partial(kernel, n_dom, n_sub, norm_factor), out_...  48.2 us
    pallas_call x1, Pallas kernels, shards(): pl.pallas_call(put, out_shape=tuple((jax.ShapeDtypeStruct(x.shape, x.dtyp...  1.17 us

profile of v5, /device:TPU:1, one launch (start us, length us, event | category | flops | bytes accessed | tf_op | source)
XLA Modules:
  0.0 50.6 jit_solution(12299658416909375763)
XLA Ops:
  1.3 48.2 %shard_map.139 = (bf16[1024,256]{1,0:T(8,128)(2,1)S(1)}, f32[1024,256]{1,0:T(8,128)S(1)}, f32[1,256]{1,0:T(1,128)S(1)}) custom-call(s32[1,1]{1,0:T(1,128)} %bitcast.8.count_hbm, s32[1,2048]{1,0:T(1,128)} %src_hbm.1, s32[1,2048]{1,0:T(1,128)} %dst_hbm.1, s32[4,128]{1,0:T(4,128)} %bitcast.10, s32[1,1024]{1,0:T(1,128)} %bitcast.9, f32[1,256]{1,0:T(1,128)} %bitcast.11, ...), custom_call_target="tpu_custom_call" | custom-call | tf_op jit(solution)/shard_map/pallas_call | solution.py:526
  49.4 1.2 %shard_map.140 = (bf16[1024,256]{1,0:T(8,128)(2,1)}, f32[1024,256]{1,0:T(8,128)}, f32[1,256]{1,0:T(1,128)}) custom-call(bf16[1024,256]{1,0:T(8,128)(2,1)S(1)} %get-tuple-element.9.refs_0_, f32[1024,256]{1,0:T(8,128)S(1)} %get-tuple-element.10.refs_1_, f32[1,256]{1,0:T(1,128)S(1)} %get-tuple-element.11.refs_2_), custom_call_target="tpu_custom_call" | custom-call | tf_op jit(solution)/shard_map/pallas_call | solution.py:603

commit v6 on v5

--- a/solution.py
+++ b/solution.py
@@ -244,6 +244,15 @@
 
         lax.fori_loop(0, slots // blk, hot, 0)
 
+    masters = nodes // blk
+    with scope("buildf"):
+
+        def build_rows(i, _):
+            rows(adj, i)[...] = nt(rows(dst_hot, i)[...], src_hot[...]).astype(BF16)
+            return 0
+
+        lax.fori_loop(masters, masters + 1, build_rows, 0)
+
     with scope("bwait"):
         pl.semaphore_wait(barrier, n_dev - 1)
     exchange(0)
@@ -258,14 +267,9 @@
         fill(1, nn(picks[...], ybuf[...]))
     exchange(1)
 
-    masters = nodes // blk
     with scope("buildm"):
 
-        def build_rows(i, _):
-            rows(adj, i)[...] = nt(rows(dst_hot, i)[...], src_hot[...]).astype(BF16)
-            return 0
-
-        lax.fori_loop(masters, slots // blk, build_rows, 0)
+        lax.fori_loop(masters + 1, slots // blk, build_rows, 0)
 
         def build_columns(i, _):
             here = pl.ds(pl.multiple_of(i * blk, blk), blk)

time: 50.7 us -> 50.8 us (level)
  no operation moved by 1% of the time
where the time goes in v6:
time: 50.8 us; the launch traced here: 50.7 us
  Pallas kernels  49.4 us (97%)
  between operations  1.29 us (3%)
    pallas_call x1, Pallas kernels, shards(): pl.pallas_call(functools.partial(kernel, n_dom, n_sub, norm_factor), out_...  48.3 us
    pallas_call x1, Pallas kernels, shards(): pl.pallas_call(put, out_shape=tuple((jax.ShapeDtypeStruct(x.shape, x.dtyp...  1.17 us

profile of v6, /device:TPU:1, one launch (start us, length us, event | category | flops | bytes accessed | tf_op | source)
XLA Modules:
  0.0 50.7 jit_solution(6523049044443984570)
XLA Ops:
  1.3 48.3 %shard_map.139 = (bf16[1024,256]{1,0:T(8,128)(2,1)S(1)}, f32[1024,256]{1,0:T(8,128)S(1)}, f32[1,256]{1,0:T(1,128)S(1)}) custom-call(s32[1,1]{1,0:T(1,128)} %bitcast.8.count_hbm, s32[1,2048]{1,0:T(1,128)} %src_hbm.1, s32[1,2048]{1,0:T(1,128)} %dst_hbm.1, s32[4,128]{1,0:T(4,128)} %bitcast.10, s32[1,1024]{1,0:T(1,128)} %bitcast.9, f32[1,256]{1,0:T(1,128)} %bitcast.11, ...), custom_call_target="tpu_custom_call" | custom-call | tf_op jit(solution)/shard_map/pallas_call | solution.py:530
  49.5 1.2 %shard_map.140 = (bf16[1024,256]{1,0:T(8,128)(2,1)}, f32[1024,256]{1,0:T(8,128)}, f32[1,256]{1,0:T(1,128)}) custom-call(bf16[1024,256]{1,0:T(8,128)(2,1)S(1)} %get-tuple-element.9.refs_0_, f32[1024,256]{1,0:T(8,128)S(1)} %get-tuple-element.10.refs_1_, f32[1,256]{1,0:T(1,128)S(1)} %get-tuple-element.11.refs_2_), custom_call_target="tpu_custom_call" | custom-call | tf_op jit(solution)/shard_map/pallas_call | solution.py:607
